TPU v7x, 32 devices: a whole 2x2x4 slice. The times are simulated.
32 devices in a mesh: rep: 2 (over y), cell: 4 (over z), sub: 4 (over x, core).
Axes of the slice: x: 2, y: 2, z: 4, core: 2. Of those that a mesh axis runs over, the one named last changes fastest.
Arguments:
- descriptors: bfloat16 [8, 4, 128, 128], P(('rep', 'cell'), 'sub'), parts along dimension 0, may hold values from -6 to 6
- positions: float32 [3, 8, 4, 128], P(None, ('rep', 'cell'), 'sub'), parts along dimension 1, may hold values from 0 to 4, as said below
- species: int32 [8, 4, 128], P(('rep', 'cell'), 'sub'), parts along dimension 0, may hold values from 0 to 3
- counts: int32 [8, 4], P(('rep', 'cell'), 'sub'), parts along dimension 0, may hold values from 80 to 128, as said below
- w_in: bfloat16 [8, 128, 256], replicated, may hold values from -0.5 to 0.5
- b_in: float32 [8, 256], replicated, may hold values from -3 to 3
- w_hid: bfloat16 [8, 256, 256], replicated, may hold values from -0.375 to 0.375
- b_hid: float32 [8, 256], replicated, may hold values from -3 to 3
- w_out: bfloat16 [8, 2, 256], replicated, may hold values from -0.375 to 0.375
Outputs:
- charges: float32 [8, 8, 4, 128], P(None, ('rep', 'cell'), 'sub'), parts along dimension 1
There are 2 independent parts, one for each index of `rep`. A program takes and returns all parts, laid end to end along the dimension named above; an argument that names none is the same for every part. Nothing has to cross between parts.
Inputs may be any that keep to these rules, and one draw needn't show every extreme that they name: `positions`: the first two coordinates of a slot lie between its cell's indices and one more, the height between 0 and 1. `counts`: a cell's slots from its count up are empty.
All inputs are finite; a program needn't handle non-finite values.
Results may differ from a plain program's by a relative error of at most 0.0003.
The roundings to bfloat16 on the way count: a program that leaves them out, or rounds other values in their place, can miss the bound.
Values sent between devices are 32-bit elements; how exact they have to be, the bound alone decides.
No kernel may reach another device: no remote copies, remote signals or barrier semaphores. Data moves between devices by JAX's collectives and lax.ppermute only.
A program may use at most 64 MiB of HBM per device.

v0:
```python
import jax
import jax.numpy as jnp
from jax import lax
from jax.sharding import PartitionSpec as P

ITERS = 2


def extended_2(shard, sides, width):
    for axis, dim in sides:
        size, length = (lax.axis_size(axis), shard.shape[dim])
        up = [(i, (i + 1) % size) for i in range(size - 1)]
        down = [(j, i) for i, j in up]
        last = lax.slice_in_dim(shard, length - width, length, axis=dim)
        leading = lax.slice_in_dim(shard, 0, width, axis=dim)
        before = lax.ppermute(last, axis, up)
        after = lax.ppermute(leading, axis, down)
        shard = jnp.concatenate([before, shard, after], axis=dim)
    return shard


def lookup(species, entries):
    choices_table = jnp.array(entries, jnp.float32)
    kinds = jnp.arange(4, dtype=jnp.int32)
    return jnp.sum((species[..., None] == kinds).astype(jnp.float32) * choices_table, axis=-1)


def coupling(own_atoms, far_atoms, self_cell):
    delta_a = own_atoms[0][..., :, None] - far_atoms[0][..., None, :]
    delta_b = own_atoms[1][..., :, None] - far_atoms[1][..., None, :]
    delta_c = own_atoms[2][..., :, None] - far_atoms[2][..., None, :]
    distance_sq = delta_a * delta_a + delta_b * delta_b + delta_c * delta_c
    radius = jnp.sqrt(distance_sq + 1e-06)
    pair_width = jnp.sqrt(own_atoms[3][..., :, None] ** 2 + far_atoms[3][..., None, :] ** 2)
    smooth_cut = (1.0 - jnp.minimum(distance_sq, 1.0)) ** 3
    kernel = 0.005 * smooth_cut * jax.scipy.special.erf(radius / pair_width) / radius
    kernel = kernel * own_atoms[4][..., :, None] * far_atoms[4][..., None, :]
    if self_cell:
        kernel = kernel * (1.0 - jnp.eye(kernel.shape[-1], dtype=jnp.float32))
    return kernel


def committee(flat_rows, w_in, b_in, w_hid, b_hid, w_out):

    def member_fn(weights):
        first_w, first_b, second_w, second_b, last_w = weights
        first = jnp.tanh(
            jnp.dot(flat_rows, first_w, preferred_element_type=jnp.float32) + first_b
        ).astype(jnp.bfloat16)
        second = jnp.tanh(
            jnp.dot(first, second_w, preferred_element_type=jnp.float32) + second_b
        ).astype(jnp.bfloat16)
        return jnp.dot(second, last_w.T, preferred_element_type=jnp.float32).T

    return lax.map(member_fn, (w_in, b_in, w_hid, b_hid, w_out))


def expand(values):
    return values[:, None, None, None]


def extend(vectors):
    return extended_2(vectors, (("cell", 1), ("sub", 2)), 1)


def two_products(residual, image_vec):
    return lax.psum(
        (
            jnp.sum(residual * residual, axis=(1, 2, 3)),
            jnp.sum(residual * image_vec, axis=(1, 2, 3)),
        ),
        ("cell", "sub"),
    )


def body(descriptors, positions, species, counts, w_in, b_in, w_hid, b_hid, w_out):
    rows_a, rows_b, slot_count, features = descriptors.shape
    members = w_in.shape[0]
    slot_iota = lax.broadcasted_iota(jnp.int32, (rows_a, rows_b, slot_count), 2)
    occupancy = (slot_iota < counts[:, :, None]).astype(jnp.float32)
    widths = lookup(species, (0.3, 0.4, 0.5, 0.35))
    shifts = lookup(species, (-0.8, 0.4, 1.2, -0.3))
    atom_data = jnp.stack([positions[0], positions[1], positions[2], widths, occupancy])
    extended = extended_2(atom_data, (("cell", 1), ("sub", 2)), 1)
    outputs = committee(descriptors.reshape(-1, features), w_in, b_in, w_hid, b_hid, w_out)
    electro = outputs[:, 0].reshape(members, rows_a, rows_b, slot_count) + shifts
    hardness = 2.5 + jax.nn.softplus(outputs[:, 1]).reshape(members, rows_a, rows_b, slot_count)
    right_side = jnp.concatenate([-electro * occupancy, jnp.broadcast_to(occupancy, electro.shape)])
    diagonal = jnp.concatenate([hardness, hardness])
    offsets = [(row_step, col_step) for row_step in (-1, 0, 1) for col_step in (-1, 0, 1)]

    def neighbours(grown, row_step, col_step):
        return grown[:, 1 + row_step : 1 + row_step + rows_a, 1 + col_step : 1 + col_step + rows_b]

    def block_for(row_step, col_step):
        return coupling(
            atom_data, neighbours(extended, row_step, col_step), row_step == 0 and col_step == 0
        )

    def operate(vectors):
        grown = extend(vectors)
        summed = diagonal * vectors
        for offset_number in range(9):
            row_step, col_step = offsets[offset_number]
            tile_block = block_for(row_step, col_step)
            summed = summed + jnp.einsum(
                "abij,rabj->rabi",
                tile_block,
                neighbours(grown, row_step, col_step),
                precision=lax.Precision.HIGHEST,
            )
        return summed

    solution = jnp.zeros_like(right_side)
    residual = right_side
    image_vec = operate(residual)
    norm_now, product = two_products(residual, image_vec)
    step_size = norm_now / product
    direction = residual
    along = image_vec
    for iteration in range(ITERS):
        solution = solution + expand(step_size) * direction
        residual = residual - expand(step_size) * along
        if iteration + 1 < ITERS:
            image_vec = operate(residual)
            norm_next, product = two_products(residual, image_vec)
            momentum = norm_next / norm_now
            step_size = norm_next / (product - momentum * norm_next / step_size)
            direction = residual + expand(momentum) * direction
            along = image_vec + expand(momentum) * along
            norm_now = norm_next
    source_part = solution[:members]
    unit_part = solution[members:]
    source_total, unit_total = lax.psum(
        (jnp.sum(source_part, axis=(1, 2, 3)), jnp.sum(unit_part, axis=(1, 2, 3))), ("cell", "sub")
    )
    multiplier = source_total / unit_total
    return source_part - expand(multiplier) * unit_part


def solution(mesh):
    placed = (
        P(("rep", "cell"), "sub", None, None),
        P(None, ("rep", "cell"), "sub", None),
        P(("rep", "cell"), "sub", None),
        P(("rep", "cell"), "sub"),
        P(),
        P(),
        P(),
        P(),
        P(),
    )
    return jax.shard_map(
        body,
        mesh=mesh,
        in_specs=placed,
        out_specs=P(None, ("rep", "cell"), "sub", None),
        check_vma=False,
    )
```

profile of v0, /device:TPU:0, one launch (start us, length us, event | category | flops | bytes accessed | tf_op | source)
XLA Modules:
  0.0 162.4 jit_solution(817328596570709719)
XLA Ops:
  0.7 24.5 %while.10 = (s32[]{:T(128)}, f32[8,2,128]{2,0,1:T(8,128)S(1)}, bf16[8,2,256]{2,1,0:T(2,128)(2,1)}, bf16[8,128,256]{2,1,0:T(8,128)(2,1)}, bf16[128,128]{1,0:T(8,1...) while((s32[]{:T(128)}, f32[8,2,128]{2,0,1:T(8,128)S(1)}, ...), condition=%wide.region_1.0_spmd, body=%wide.region_0.0_spmd.sunk | while | flops 25427968 | bytes 372333 | solution.py:55
  1.4 1.0 fusion.170
  2.5 1.2 fusion.171
  5.5 1.2 fusion.171
  7.5 1.0 fusion.170
  8.6 1.2 fusion.171
  10.6 1.0 fusion.170
  11.6 1.2 fusion.171
  13.6 1.0 fusion.170
  14.7 1.2 fusion.171
  16.7 1.0 fusion.170
  17.7 1.2 fusion.171
  19.7 1.0 fusion.170
  20.8 1.2 fusion.171
  23.8 1.2 fusion.171
  26.1 4.9 %collective-permute-start = (f32[16,1,1,128]{3,0,2,1:T(8,128)S(1)}, f32[16,1,1,128]{3,0,2,1:T(8,128)S(1)}, u32[]{:S(2)}, u32[]{:S(2)}) collective-permute-start(f32[16,1,1,128]{3,0,2,1:T(8,128)S(1)} %get-tuple-element.113), channel_id=1, source_target_pairs={{0,4},{4,8},{8,12},{1,5},{5,9},{9,13},{2,6},{6,10},{10,14},{3,7},{... | collective-permute-start | bytes 24584 | tf_op jit(solution)/shard_map/ppermute | solution.py:16
  31.0 1.3 collective-permute-start.1
  33.0 4.5 %collective-permute-start.3 = (f32[5,1,1,128]{3,2,1,0:T(1,128)S(1)}, f32[5,1,1,128]{3,2,1,0:T(1,128)S(1)}, u32[]{:S(2)}, u32[]{:S(2)}) collective-permute-start(f32[5,1,1,128]{3,2,1,0:T(1,128)S(1)} %pad_maximum_fusion.7), channel_id=1, source_target_pairs={{0,4},{4,8},{8,12},{1,5},{5,9},{9,13},{2,6},{6,10},{10,14},{3,7},{... | collective-permute-start | bytes 7688 | tf_op jit(solution)/shard_map/ppermute | solution.py:16
  37.5 1.3 collective-permute-start.4
  39.2 3.8 %collective-permute-done.4 = f32[5,1,1,128]{3,2,1,0:T(1,128)S(1)} collective-permute-done((f32[5,1,1,128]{3,2,1,0:T(1,128)S(1)}, f32[5,1,1,128]{3,2,1,0:T(1,128)S(1)}, u32[]{:S(2)}, u32[]{:S(2)}) %collective-permute-start.4) | collective-permute-done | bytes 2592 | tf_op jit(solution)/shard_map/ppermute | solution.py:17
  43.0 1.3 collective-permute-start.7
  44.3 3.0 %collective-permute-start.5 = (f32[5,3,1,128]{3,2,1,0:T(1,128)S(1)}, f32[5,3,1,128]{3,2,1,0:T(1,128)S(1)}, u32[]{:S(2)}, u32[]{:S(2)}) collective-permute-start(f32[5,3,1,128]{3,2,1,0:T(1,128)S(1)} %pad_maximum_fusion.6), channel_id=1, source_target_pairs={{0,1},{1,2},{2,3},{4,5},{5,6},{6,7},{8,9},{9,10},{10,11},{12,13},{... | collective-permute-start | bytes 23048 | tf_op jit(solution)/shard_map/ppermute | solution.py:16
  47.4 1.3 collective-permute-start.6
  48.7 3.6 %collective-permute-start.2 = (f32[16,3,1,128]{3,0,2,1:T(8,128)S(1)}, f32[16,3,1,128]{3,0,2,1:T(8,128)S(1)}, u32[]{:S(2)}, u32[]{:S(2)}) collective-permute-start(f32[16,3,1,128]{3,0,2,1:T(8,128)S(1)} %pad_maximum_fusion), channel_id=1, source_target_pairs={{0,1},{1,2},{2,3},{4,5},{5,6},{6,7},{8,9},{9,10},{10,11},{12,13},{... | collective-permute-start | bytes 73736 | tf_op jit(solution)/shard_map/ppermute | solution.py:16
  55.5 32.3 %all-reduce.2 = (f32[16]{0:T(128)S(1)}, f32[16]{0:T(128)S(1)}) all-reduce(f32[16]{0:T(128)S(1)} %get-tuple-element.112, f32[16]{0:T(128)S(1)} %get-tuple-element.127), channel_id=1, replica_groups=mesh['rep'=2,'cell'=4,'sub'=4] {'cell','sub'}, use_global_device_ids=true, to_apply=%region_4.5 | all-reduce | flops 32 | bytes 256 | tf_op jit(solution)/shard_map/psum | solution.py:67
  87.9 1.3 collective-permute-start.8
  89.2 1.3 collective-permute-start.9
  90.9 3.9 %collective-permute-done.9 = f32[16,1,1,128]{3,0,2,1:T(8,128)S(1)} collective-permute-done((f32[16,1,1,128]{3,0,2,1:T(8,128)S(1)}, f32[16,1,1,128]{3,0,2,1:T(8,128)S(1)}, u32[]{:S(2)}, u32[]{:S(2)}) %collective-permute-start.9) | collective-permute-done | bytes 8224 | tf_op jit(solution)/shard_map/ppermute | solution.py:17
  94.8 1.3 collective-permute-start.11
  96.1 3.0 %collective-permute-start.10 = (f32[16,3,1,128]{3,0,2,1:T(8,128)S(1)}, f32[16,3,1,128]{3,0,2,1:T(8,128)S(1)}, u32[]{:S(2)}, u32[]{:S(2)}) collective-permute-start(f32[16,3,1,128]{3,0,2,1:T(8,128)S(1)} %pad_maximum_fusion.1), channel_id=1, source_target_pairs={{0,1},{1,2},{2,3},{4,5},{5,6},{6,7},{8,9},{9,10},{10,11},{12,13},{... | collective-permute-start | bytes 73736 | tf_op jit(solution)/shard_map/ppermute | solution.py:16
  102.2 29.8 %all-reduce.1 = (f32[16]{0:T(128)S(1)}, f32[16]{0:T(128)S(1)}) all-reduce(f32[16]{0:T(128)S(1)} %get-tuple-element.76, f32[16]{0:T(128)S(1)} %fusion.32), channel_id=1, replica_groups=mesh['rep'=2,'cell'=4,'sub'=4] {'cell','sub'}, use_global_device_ids=true, to_apply=%region_9.10 | all-reduce | flops 32 | bytes 256 | tf_op jit(solution)/shard_map/psum | solution.py:67
  132.3 29.5 %all-reduce = (f32[8]{0:T(128)S(1)}, f32[8]{0:T(128)S(1)}) all-reduce(f32[8]{0:T(128)S(1)} %get-tuple-element.49, f32[8]{0:T(128)S(1)} %get-tuple-element.48), channel_id=1, replica_groups=mesh['rep'=2,'cell'=4,'sub'=4] {'cell','sub'}, use_global_device_ids=true, to_apply=%region_13.14 | all-reduce | flops 16 | bytes 128 | tf_op jit(solution)/shard_map/psum | solution.py:134
  (80 shorter events, 17.5 us)
Async XLA Ops:
  25.1 0.7 copy-start.1
  25.1 0.7 copy-start.2
  25.1 0.7 copy-start.3
  26.1 21.3 %collective-permute-start = (f32[16,1,1,128]{3,0,2,1:T(8,128)S(1)}, f32[16,1,1,128]{3,0,2,1:T(8,128)S(1)}, u32[]{:S(2)}, u32[]{:S(2)}) collective-permute-start(f32[16,1,1,128]{3,0,2,1:T(8,128)S(1)} %get-tuple-element.113), channel_id=1, source_target_pairs={{0,4},{4,8},{8,12},{1,5},{5,9},{9,13},{2,6},{6,10},{10,14},{3,7},{... | collective-permute-start | bytes 24584 | tf_op jit(solution)/shard_map/ppermute | solution.py:16
  31.0 16.4 %collective-permute-start.1 = (f32[16,1,1,128]{3,0,2,1:T(8,128)S(1)}, f32[16,1,1,128]{3,0,2,1:T(8,128)S(1)}, u32[]{:S(2)}, u32[]{:S(2)}) collective-permute-start(f32[16,1,1,128]{3,0,2,1:T(8,128)S(1)} %get-tuple-element.113), channel_id=1, source_target_pairs={{4,0},{8,4},{12,8},{5,1},{9,5},{13,9},{6,2},{10,6},{14,10},{7,3},{... | collective-permute-start | bytes 24584 | tf_op jit(solution)/shard_map/ppermute | solution.py:17
  32.3 0.7 copy-start
  33.0 6.2 %collective-permute-start.3 = (f32[5,1,1,128]{3,2,1,0:T(1,128)S(1)}, f32[5,1,1,128]{3,2,1,0:T(1,128)S(1)}, u32[]{:S(2)}, u32[]{:S(2)}) collective-permute-start(f32[5,1,1,128]{3,2,1,0:T(1,128)S(1)} %pad_maximum_fusion.7), channel_id=1, source_target_pairs={{0,4},{4,8},{8,12},{1,5},{5,9},{9,13},{2,6},{6,10},{10,14},{3,7},{... | collective-permute-start | bytes 7688 | tf_op jit(solution)/shard_map/ppermute | solution.py:16
  37.5 5.5 %collective-permute-start.4 = (f32[5,1,1,128]{3,2,1,0:T(1,128)S(1)}, f32[5,1,1,128]{3,2,1,0:T(1,128)S(1)}, u32[]{:S(2)}, u32[]{:S(2)}) collective-permute-start(f32[5,1,1,128]{3,2,1,0:T(1,128)S(1)} %pad_maximum_fusion.7), channel_id=1, source_target_pairs={{4,0},{8,4},{12,8},{5,1},{9,5},{13,9},{6,2},{10,6},{14,10},{7,3},{... | collective-permute-start | bytes 7688 | tf_op jit(solution)/shard_map/ppermute | solution.py:17
  43.0 10.0 %collective-permute-start.7 = (f32[5,3,1,128]{3,2,1,0:T(1,128)S(1)}, f32[5,3,1,128]{3,2,1,0:T(1,128)S(1)}, u32[]{:S(2)}, u32[]{:S(2)}) collective-permute-start(f32[5,3,1,128]{3,2,1,0:T(1,128)S(1)} %pad_maximum_fusion.6), channel_id=1, source_target_pairs={{1,0},{2,1},{3,2},{5,4},{6,5},{7,6},{9,8},{10,9},{11,10},{13,12},{... | collective-permute-start | bytes 23048 | tf_op jit(solution)/shard_map/ppermute | solution.py:17
  44.3 8.8 %collective-permute-start.5 = (f32[5,3,1,128]{3,2,1,0:T(1,128)S(1)}, f32[5,3,1,128]{3,2,1,0:T(1,128)S(1)}, u32[]{:S(2)}, u32[]{:S(2)}) collective-permute-start(f32[5,3,1,128]{3,2,1,0:T(1,128)S(1)} %pad_maximum_fusion.6), channel_id=1, source_target_pairs={{0,1},{1,2},{2,3},{4,5},{5,6},{6,7},{8,9},{9,10},{10,11},{12,13},{... | collective-permute-start | bytes 23048 | tf_op jit(solution)/shard_map/ppermute | solution.py:16
  47.4 6.5 %collective-permute-start.6 = (f32[16,3,1,128]{3,0,2,1:T(8,128)S(1)}, f32[16,3,1,128]{3,0,2,1:T(8,128)S(1)}, u32[]{:S(2)}, u32[]{:S(2)}) collective-permute-start(f32[16,3,1,128]{3,0,2,1:T(8,128)S(1)} %pad_maximum_fusion), channel_id=1, source_target_pairs={{1,0},{2,1},{3,2},{5,4},{6,5},{7,6},{9,8},{10,9},{11,10},{13,12},{... | collective-permute-start | bytes 73736 | tf_op jit(solution)/shard_map/ppermute | solution.py:17
  48.7 4.5 %collective-permute-start.2 = (f32[16,3,1,128]{3,0,2,1:T(8,128)S(1)}, f32[16,3,1,128]{3,0,2,1:T(8,128)S(1)}, u32[]{:S(2)}, u32[]{:S(2)}) collective-permute-start(f32[16,3,1,128]{3,0,2,1:T(8,128)S(1)} %pad_maximum_fusion), channel_id=1, source_target_pairs={{0,1},{1,2},{2,3},{4,5},{5,6},{6,7},{8,9},{9,10},{10,11},{12,13},{... | collective-permute-start | bytes 73736 | tf_op jit(solution)/shard_map/ppermute | solution.py:16
  87.9 2.9 %collective-permute-start.8 = (f32[16,1,1,128]{3,0,2,1:T(8,128)S(1)}, f32[16,1,1,128]{3,0,2,1:T(8,128)S(1)}, u32[]{:S(2)}, u32[]{:S(2)}) collective-permute-start(f32[16,1,1,128]{3,0,2,1:T(8,128)S(1)} %bitcast.216), channel_id=1, source_target_pairs={{0,4},{4,8},{8,12},{1,5},{5,9},{9,13},{2,6},{6,10},{10,14},{3,7},{... | collective-permute-start | bytes 24584 | tf_op jit(solution)/shard_map/ppermute | solution.py:16
  89.2 5.5 %collective-permute-start.9 = (f32[16,1,1,128]{3,0,2,1:T(8,128)S(1)}, f32[16,1,1,128]{3,0,2,1:T(8,128)S(1)}, u32[]{:S(2)}, u32[]{:S(2)}) collective-permute-start(f32[16,1,1,128]{3,0,2,1:T(8,128)S(1)} %bitcast.217), channel_id=1, source_target_pairs={{4,0},{8,4},{12,8},{5,1},{9,5},{13,9},{6,2},{10,6},{14,10},{7,3},{... | collective-permute-start | bytes 24584 | tf_op jit(solution)/shard_map/ppermute | solution.py:17
  94.8 5.8 %collective-permute-start.11 = (f32[16,3,1,128]{3,0,2,1:T(8,128)S(1)}, f32[16,3,1,128]{3,0,2,1:T(8,128)S(1)}, u32[]{:S(2)}, u32[]{:S(2)}) collective-permute-start(f32[16,3,1,128]{3,0,2,1:T(8,128)S(1)} %pad_maximum_fusion.1), channel_id=1, source_target_pairs={{1,0},{2,1},{3,2},{5,4},{6,5},{7,6},{9,8},{10,9},{11,10},{13,12},{... | collective-permute-start | bytes 73736 | tf_op jit(solution)/shard_map/ppermute | solution.py:17
  96.1 3.9 %collective-permute-start.10 = (f32[16,3,1,128]{3,0,2,1:T(8,128)S(1)}, f32[16,3,1,128]{3,0,2,1:T(8,128)S(1)}, u32[]{:S(2)}, u32[]{:S(2)}) collective-permute-start(f32[16,3,1,128]{3,0,2,1:T(8,128)S(1)} %pad_maximum_fusion.1), channel_id=1, source_target_pairs={{0,1},{1,2},{2,3},{4,5},{5,6},{6,7},{8,9},{9,10},{10,11},{12,13},{... | collective-permute-start | bytes 73736 | tf_op jit(solution)/shard_map/ppermute | solution.py:16
where the time goes:
time: 164 us; the launch traced here: 162 us
  blocking collectives  91.6 us (56%)
  starting transfers between devices  28.2 us (17%)
  matrix products  24.6 us (15%)
  waiting for transfers between devices  8.07 us (5%)
  local copies, waits for them, and re-layouts  7.33 us (4%)
    psum x2, blocking collectives, two_products(): lax.psum((jnp.sum(residual * residual, axis=(1, 2, 3)), jnp.sum(residual...  62.1 us
    psum x1, blocking collectives, body(): lax.psum((jnp.sum(source_part, axis=(1, 2, 3)), jnp.sum(unit_part, axis=(...  29.5 us
    ppermute x6, starting transfers between devices, extended_2(): before = lax.ppermute(last, axis, up)  20.5 us
    dot_general x8, matrix products, member_fn(): return jnp.dot(second, last_w.T, preferred_element_type=jnp.float32).T  9.96 us
    dot_general x8, matrix products, member_fn(): jnp.dot(flat_rows, first_w, preferred_element_type=jnp.float32) + first_b  8.33 us
    ppermute x6, waiting for transfers between devices, extended_2(): after = lax.ppermute(leading, axis, down)  7.78 us
    ppermute x6, starting transfers between devices, extended_2(): after = lax.ppermute(leading, axis, down)  7.74 us
    dot_general x18, matrix products, operate(): jnp.einsum('abij,rabj->rabi', tile_block, neighbours(grown, row_step, col...  6.36 us
  transfers between devices with their start and end apart: 12, of which 4 were waited for; matrix products, arithmetic and copies ran while one was open for 2% of the time, Pallas kernels for 0%

commit v1 on v0

--- a/solution.py
+++ b/solution.py
@@ -1,9 +1,259 @@
 import jax
 import jax.numpy as jnp
 from jax import lax
+from jax.experimental import pallas as pl
+from jax.experimental.pallas import tpu as pltpu
 from jax.sharding import PartitionSpec as P
 
 ITERS = 2
+
+ERF_CENTRE = 1.000001 / 0.36
+ERF_SERIES = (
+    0.5889464636197189,
+    -0.09338177281045029,
+    0.018898799573350084,
+    -0.003564793815999453,
+    0.0005967292996019212,
+    -8.816834134949323e-05,
+    1.1544704937919275e-05,
+    -1.3330679803919568e-06,
+    1.4072010724176845e-07,
+    -1.592848428884591e-08,
+    1.4031096882113396e-09,
+)
+
+HARD, PLACE, SPREAD, FULL, ROWS = 8, 16, 19, 20, 24
+OFFSETS = ((0, 0), (0, 1), (1, -1), (1, 0), (1, 1))
+MOST_BLOCKS = 128
+
+
+def pair_counts(rows, cols):
+    return [(rows - da) * (cols - abs(db)) for da, db in OFFSETS]
+
+
+def choose(species, entries):
+    value = jnp.full(species.shape, entries[3], jnp.float32)
+    for kind in (2, 1, 0):
+        value = jnp.where(species == kind, entries[kind], value)
+    return value
+
+
+def slab_kernel(
+    desc_ref, pos_ref, species_ref, counts_ref, w_in, b_in, w_hid, b_hid, w_out, out_ref
+):
+    members = w_in.shape[0]
+    slots = desc_ref.shape[0]
+    species = species_ref[0]
+    slot_iota = lax.broadcasted_iota(jnp.int32, (1, slots), 1)
+    occupancy = (slot_iota < counts_ref[0, 0]).astype(jnp.float32)
+    widths = choose(species, (0.3, 0.4, 0.5, 0.35))
+    shifts = choose(species, (-0.8, 0.4, 1.2, -0.3))
+    rows = desc_ref[...]
+    electro, raw = [], []
+    for m in range(members):
+        first = jnp.tanh(
+            jnp.dot(rows, w_in[m], preferred_element_type=jnp.float32) + b_in[m : m + 1, :]
+        ).astype(jnp.bfloat16)
+        second = jnp.tanh(
+            jnp.dot(first, w_hid[m], preferred_element_type=jnp.float32) + b_hid[m : m + 1, :]
+        ).astype(jnp.bfloat16)
+        outputs = lax.dot_general(
+            w_out[m], second, (((1,), (1,)), ((), ())), preferred_element_type=jnp.float32
+        )
+        electro.append(outputs[0:1])
+        raw.append(outputs[1:2])
+    raw = jnp.concatenate(raw, axis=0)
+    hardness = 2.5 + (jnp.maximum(raw, 0.0) + jnp.log1p(jnp.exp(-jnp.abs(raw))))
+    right = -(jnp.concatenate(electro, axis=0) + shifts) * occupancy
+    atoms = jnp.concatenate(
+        [pos_ref[0, 0], pos_ref[1, 0], pos_ref[2, 0], widths * widths, occupancy]
+        + [jnp.zeros((1, slots), jnp.float32)] * (ROWS - FULL - 1),
+        axis=0,
+    )
+    for peer in range(out_ref.shape[0]):
+        out_ref[peer, 0:HARD, :] = right
+        out_ref[peer, HARD:PLACE, :] = hardness
+        out_ref[peer, PLACE:ROWS, :] = atoms
+
+
+def pair_block(cols, slab_ref, c, d, first_row, height, own):
+    span = pl.ds(first_row, height)
+
+    def gap(k):
+        return cols[c, span, k : k + 1] - slab_ref[d, PLACE + k : PLACE + k + 1, :]
+
+    da, db, dc = gap(0), gap(1), gap(2)
+    capped = jnp.minimum(da * da + db * db + dc * dc, 1.0)
+    left = 1.0 - capped
+    inv = lax.rsqrt(cols[c, span, 3:4] + slab_ref[d, SPREAD : SPREAD + 1, :])
+    y = (capped + 1e-06) * (inv * inv) - ERF_CENTRE
+    value = jnp.full_like(y, 0.005 * ERF_SERIES[-1])
+    for term in ERF_SERIES[-2::-1]:
+        value = value * y + 0.005 * term
+    value = value * ((left * inv) * (left * left))
+    if own:
+        i = lax.broadcasted_iota(jnp.int32, value.shape, 0) + first_row
+        j = lax.broadcasted_iota(jnp.int32, value.shape, 1)
+        value = jnp.where(i == j, 0.0, value)
+    return value
+
+
+def times(vectors, block):
+    return jnp.dot(vectors, block, preferred_element_type=jnp.float32)
+
+
+def times_t(vectors, block):
+    return lax.dot_general(
+        vectors, block, (((1,), (1,)), ((), ())), preferred_element_type=jnp.float32
+    )
+
+
+def halves(values):
+    high = values.astype(jnp.bfloat16)
+    return high, (values - high.astype(jnp.float32)).astype(jnp.bfloat16)
+
+
+def solve_kernel(grid, slab_ref, out_ref, cols, vecs, sums, resid, resid_half, k_high, k_low):
+    rows, columns = grid
+    cells, _, slots = slab_ref.shape
+    members = HARD
+    starts = [0]
+    for count in pair_counts(rows, columns):
+        starts.append(starts[-1] + count)
+
+    for c in range(cells):
+        cols[c] = slab_ref[c, PLACE:ROWS, :].T
+        high, low = halves(slab_ref[c, 0:HARD, :])
+        vecs[c, 0:16, :] = jnp.concatenate([high.astype(jnp.float32), low.astype(jnp.float32)], axis=0).astype(jnp.bfloat16)
+        full = slab_ref[c, FULL : FULL + 1, :]
+        row = lax.broadcasted_iota(jnp.int32, (16, slots), 0)
+        vecs[c, 16:32, :] = jnp.where(row == 0, full, 0.0).astype(jnp.bfloat16)
+        sums[c] = jnp.zeros_like(sums[c])
+
+    def each_pair(handle):
+        for number, (da, db) in enumerate(OFFSETS):
+            low_col = max(0, -db)
+            width = columns - abs(db)
+
+            def line(a, carry, number=number, da=da, db=db, low_col=low_col, width=width):
+                for step in range(width):
+                    c = a * columns + (low_col + step)
+                    d = (a + da) * columns + (low_col + step + db)
+                    carry = handle(c, d, starts[number] + a * width + step, number == 0, carry)
+                return carry
+
+            yield line, rows - da
+
+    def first_pass(c, d, place, own, carry):
+        for first_row in range(0, slots, 32):
+            high, low = halves(pair_block(cols, slab_ref, c, d, first_row, 32, own))
+            k_high[place, first_row : first_row + 32, :] = high
+            k_low[place, first_row : first_row + 32, :] = low
+        high, low = k_high[place], k_low[place]
+        far = vecs[d]
+        sums[c] += times_t(far, high) + times_t(far, low)
+        if not own:
+            near = vecs[c]
+            sums[d] += times(near, high) + times(near, low)
+        return carry
+
+    for line, length in each_pair(first_pass):
+        lax.fori_loop(0, length, line, 0)
+
+    def applied(c):
+        hard = slab_ref[c, HARD:PLACE, :]
+        full = slab_ref[c, FULL : FULL + 1, :]
+        right = slab_ref[c, 0:HARD, :]
+        coupled = sums[c]
+        image_s = hard * right + full * (coupled[0:8] + coupled[8:16])
+        image_u = full * (hard + coupled[16:17])
+        return hard, full, right, image_s, image_u
+
+    shape = (members, slots)
+    norm_s, prod_s, prod_u, total_s = (jnp.zeros(shape, jnp.float32) for _ in range(4))
+    norm_u = jnp.zeros((1, slots), jnp.float32)
+    for c in range(cells):
+        hard, full, right, image_s, image_u = applied(c)
+        norm_s += right * right
+        norm_u += full * full
+        prod_s += right * image_s
+        prod_u += full * image_u
+        total_s += right
+
+    def over(values):
+        return jnp.sum(values, axis=1, keepdims=True)
+
+    both = lambda s, u: jnp.concatenate([s, jnp.broadcast_to(u, s.shape)], axis=0)
+    norm0 = both(over(norm_s), over(norm_u))
+    total0 = both(over(total_s), over(norm_u))
+    alpha0 = norm0 / both(over(prod_s), over(prod_u))
+
+    norm1, prod1, total1 = (jnp.zeros((2 * members, slots), jnp.float32) for _ in range(3))
+    for c in range(cells):
+        hard, full, right, image_s, image_u = applied(c)
+        left = both(right, full) - alpha0 * jnp.concatenate([image_s, image_u], axis=0)
+        resid[c] = left
+        high, low = halves(left)
+        resid_half[c, 0:16, :] = high
+        resid_half[c, 16:32, :] = low
+        square = left * left
+        norm1 += square
+        prod1 += jnp.concatenate([hard, hard], axis=0) * square
+        total1 += left
+
+    def second_pass(c, d, place, own, carry):
+        near = resid_half[c]
+        image = times(near, k_high[place]) + times(near, k_low[place])
+        part = (image[0:16] + image[16:32]) * resid[d]
+        return carry + (part if own else 2.0 * part)
+
+    for line, length in each_pair(second_pass):
+        prod1 = lax.fori_loop(0, length, line, prod1)
+
+    norm1, prod1, total1 = over(norm1), over(prod1), over(total1)
+    momentum = norm1 / norm0
+    alpha1 = norm1 / (prod1 - momentum * norm1 / alpha0)
+    weight0 = alpha0 + alpha1 * momentum
+    totals = weight0 * total0 + alpha1 * total1
+    multiplier = totals[0:members] / totals[members:]
+    mine = lax.axis_index("cell") * columns + lax.axis_index("sub")
+    right = both(slab_ref[mine, 0:HARD, :], slab_ref[mine, FULL : FULL + 1, :])
+    answer = weight0 * right + alpha1 * resid[mine]
+    out_ref[...] = answer[0:members] - multiplier * answer[members:]
+
+
+def gathered(descriptors, positions, species, counts, w_in, b_in, w_hid, b_hid, w_out):
+    rows, columns = lax.axis_size("cell"), lax.axis_size("sub")
+    cells, slots, members = rows * columns, descriptors.shape[2], w_in.shape[0]
+    vmem = pl.BlockSpec(memory_space=pltpu.VMEM)
+    slabs = pl.pallas_call(
+        slab_kernel,
+        out_shape=jax.ShapeDtypeStruct((cells, ROWS, slots), jnp.float32),
+        in_specs=[vmem] * 3 + [pl.BlockSpec(memory_space=pltpu.SMEM)] + [vmem] * 5,
+        out_specs=vmem,
+        compiler_params=pltpu.CompilerParams(vmem_limit_bytes=32 << 20),
+        name="slab",
+    )(descriptors.reshape(slots, -1), positions, species, counts, w_in, b_in, w_hid, b_hid, w_out)
+    slabs = lax.all_to_all(slabs, ("cell", "sub"), 0, 0, tiled=True)
+    blocks = sum(pair_counts(rows, columns))
+    charges = pl.pallas_call(
+        lambda *refs: solve_kernel((rows, columns), *refs),
+        out_shape=jax.ShapeDtypeStruct((members, slots), jnp.float32),
+        in_specs=[vmem],
+        out_specs=vmem,
+        scratch_shapes=[
+            pltpu.VMEM((cells, slots, ROWS - PLACE), jnp.float32),
+            pltpu.VMEM((cells, 32, slots), jnp.bfloat16),
+            pltpu.VMEM((cells, 32, slots), jnp.float32),
+            pltpu.VMEM((cells, 16, slots), jnp.float32),
+            pltpu.VMEM((cells, 32, slots), jnp.bfloat16),
+            pltpu.VMEM((blocks, slots, slots), jnp.bfloat16),
+            pltpu.VMEM((blocks, slots, slots), jnp.bfloat16),
+        ],
+        compiler_params=pltpu.CompilerParams(vmem_limit_bytes=32 << 20),
+        name="solve",
+    )(slabs)
+    return charges.reshape(members, 1, 1, slots)
 
 
 def extended_2(shard, sides, width):
@@ -150,8 +400,9 @@
         P(),
         P(),
     )
+    rows, columns = mesh.shape["cell"], mesh.shape["sub"]
     return jax.shard_map(
-        body,
+        gathered if sum(pair_counts(rows, columns)) <= MOST_BLOCKS else body,
         mesh=mesh,
         in_specs=placed,
         out_specs=P(None, ("rep", "cell"), "sub", None),

time: 164 us -> 40.8 us (0.25)
  blocking collectives: 91.6 us -> 16.2 us
  starting transfers between devices: 28.2 us -> 0 us
  matrix products: 24.6 us -> 0 us
  Pallas kernels: 0 us -> 17.8 us
  waiting for transfers between devices: 8.07 us -> 0 us
    psum x3 -> x0, blocking collectives: 91.6 us -> none  [the longest x2 62.1 us: two_products(): lax.psum((jnp.sum(residual * residual, axis=(1, 2, 3)), jnp.sum(residual...]
    ppermute x12 -> x0, starting transfers between devices: 28.2 us -> none  [the longest x6 20.5 us: extended_2(): before = lax.ppermute(last, axis, up)]
    dot_general x34 -> x0, matrix products: 24.6 us -> none  [the longest x8 9.96 us: member_fn(): return jnp.dot(second, last_w.T, preferred_element_type=jnp.float32).T]
    pallas_call x0 -> x2, Pallas kernels: none -> 17.8 us  [the longest x1 15.6 us: gathered(): pl.pallas_call(lambda *refs: solve_kernel((rows, columns), *refs), out_sh...]
    all_to_all x0 -> x1, blocking collectives: none -> 16.2 us  [gathered(): slabs = lax.all_to_all(slabs, ('cell', 'sub'), 0, 0, tiled=True)]
    ppermute x12 -> x0, waiting for transfers between devices: 8.07 us -> none  [the longest x6 7.78 us: extended_2(): after = lax.ppermute(leading, axis, down)]
    dynamic_slice x8 -> x0, local copies, waits for them, and re-layouts: 5.8 us -> none  [committee(): return lax.map(member_fn, (w_in, b_in, w_hid, b_hid, w_out))]
    unnamed x8 -> x16, local copies, waits for them, and re-layouts: 1.34 us -> 5.75 us
  transfers between devices with their start and end apart: 12 -> 0, of which waited for: 4 -> 0; matrix products, arithmetic and copies ran while one was open for 2% -> 0% of each run, Pallas kernels for 0% -> 0%
where the time goes in v1:
time: 40.8 us; the launch traced here: 40.4 us
  Pallas kernels  17.8 us (44%)
  blocking collectives  16.2 us (40%)
  local copies, waits for them, and re-layouts  5.75 us (14%)
  between operations  0.7 us (2%)
    all_to_all x1, blocking collectives, gathered(): slabs = lax.all_to_all(slabs, ('cell', 'sub'), 0, 0, tiled=True)  16.2 us
    pallas_call x1, Pallas kernels, gathered(): pl.pallas_call(lambda *refs: solve_kernel((rows, columns), *refs), out_sh...  15.6 us
    unnamed x16, local copies, waits for them, and re-layouts  5.75 us
    pallas_call x1, Pallas kernels, gathered(): pl.pallas_call(slab_kernel, out_shape=jax.ShapeDtypeStruct((cells, ROWS,...  2.21 us

profile of v1, /device:TPU:0, one launch (start us, length us, event | category | flops | bytes accessed | tf_op | source)
XLA Modules:
  0.0 40.4 jit_solution(10400396047751528956)
XLA Ops:
  0.0 0.0 copy-start.6
  0.7 0.0 copy-start.7
  0.7 0.0 copy-done.6
  0.7 0.6 %copy-done.7 = s32[1,1,128]{2,1,0:T(1,128)S(1)} copy-done((s32[1,1,128]{2,1,0:T(1,128)S(1)}, s32[1,1,128]{2,1,0:T(1,128)}, u32[]{:S(2)}) %copy-start.7) | copy-done | bytes 536
  1.3 0.0 copy-start
  1.3 1.2 %copy-done = bf16[8,256,256]{2,1,0:T(8,128)(2,1)S(1)} copy-done((bf16[8,256,256]{2,1,0:T(8,128)(2,1)S(1)}, bf16[8,256,256]{2,1,0:T(8,128)(2,1)}, u32[]{:S(2)}) %copy-start) | copy-done | bytes 1048600
  2.6 0.0 copy-start.1
  2.6 1.0 %copy-done.1 = bf16[8,128,256]{2,1,0:T(8,128)(2,1)S(1)} copy-done((bf16[8,128,256]{2,1,0:T(8,128)(2,1)S(1)}, bf16[8,128,256]{2,1,0:T(8,128)(2,1)}, u32[]{:S(2)}) %copy-start.1) | copy-done | bytes 524312
  3.6 0.0 copy-start.2
  3.6 0.8 %copy-done.2 = bf16[1,1,128,128]{3,2,1,0:T(8,128)(2,1)S(1)} copy-done((bf16[1,1,128,128]{3,2,1,0:T(8,128)(2,1)S(1)}, bf16[1,1,128,128]{3,2,1,0:T(8,128)(2,1)}, u32[]{:S(2)}) %copy-start.2) | copy-done | bytes 32792
  4.4 0.0 copy-start.3
  4.4 0.7 %copy-done.3 = f32[8,256]{1,0:T(8,128)S(1)} copy-done((f32[8,256]{1,0:T(8,128)S(1)}, f32[8,256]{1,0:T(8,128)}, u32[]{:S(2)}) %copy-start.3) | copy-done | bytes 8216
  5.0 0.0 copy-start.4
  5.1 0.7 %copy-done.4 = f32[8,256]{1,0:T(8,128)S(1)} copy-done((f32[8,256]{1,0:T(8,128)S(1)}, f32[8,256]{1,0:T(8,128)}, u32[]{:S(2)}) %copy-start.4) | copy-done | bytes 8216
  5.7 0.0 copy-start.5
  5.7 0.7 %copy-done.5 = bf16[8,2,256]{2,1,0:T(2,128)(2,1)S(1)} copy-done((bf16[8,2,256]{2,1,0:T(2,128)(2,1)S(1)}, bf16[8,2,256]{2,1,0:T(2,128)(2,1)}, u32[]{:S(2)}) %copy-start.5) | copy-done | bytes 8216
  6.4 2.2 %slab.1 = f32[16,24,128]{2,1,0:T(8,128)S(1)} custom-call(bf16[128,128]{1,0:T(8,128)(2,1)S(1)} %bitcast.4, f32[3,1,1,128]{3,2,1,0:T(1,128)S(1)} %copy-done.6, s32[1,1,128]{2,1,0:T(1,128)S(1)} %copy-done.7, s32[1,1]{1,0:T(1,128)S(6)} %copy.11.counts_ref, bf16[8,128,256]{2,1,0:T(8,128)(2,1)S(1)} %copy-done.1, f32[8,256]{1,0:T(8,128)S(1)} %copy-done.3, ...), custom_call_target="tpu_custom_call" | custom-call | tf_op jit(solution)/shard_map/slab/pallas_call | solution.py:229
  8.7 16.2 %all_to_all.5.refs_0_ = f32[16,24,128]{2,1,0:T(8,128)S(1)} all-to-all(f32[16,24,128]{2,1,0:T(8,128)S(1)} %slab.1), channel_id=1, replica_groups=mesh['rep'=2,'cell'=4,'sub'=4] {'cell','sub'}, dimensions={0} | all-to-all | bytes 393216 | tf_op jit(solution)/shard_map/all_to_all | solution.py:237
  24.8 15.6 %solve.1 = f32[8,128]{1,0:T(8,128)} custom-call(f32[16,24,128]{2,1,0:T(8,128)S(1)} %all_to_all.5.refs_0_), custom_call_target="tpu_custom_call" | custom-call | tf_op jit(solution)/shard_map/solve/pallas_call | solution.py:239
Async XLA Ops:
  0.0 0.7 %copy-start.6 = (f32[3,1,1,128]{3,2,1,0:T(1,128)S(1)}, f32[3,1,1,128]{3,2,1,0:T(1,128)}, u32[]{:S(2)}) copy-start(f32[3,1,1,128]{3,2,1,0:T(1,128)} %pos_ref.1) | copy-start | bytes 4612
  0.7 0.7 %copy-start.7 = (s32[1,1,128]{2,1,0:T(1,128)S(1)}, s32[1,1,128]{2,1,0:T(1,128)}, u32[]{:S(2)}) copy-start(s32[1,1,128]{2,1,0:T(1,128)} %species_ref.1) | copy-start | bytes 1540
  1.3 1.2 %copy-start = (bf16[8,256,256]{2,1,0:T(8,128)(2,1)S(1)}, bf16[8,256,256]{2,1,0:T(8,128)(2,1)}, u32[]{:S(2)}) copy-start(bf16[8,256,256]{2,1,0:T(8,128)(2,1)} %w_hid.1) | copy-start | bytes 3145732
  2.6 1.0 %copy-start.1 = (bf16[8,128,256]{2,1,0:T(8,128)(2,1)S(1)}, bf16[8,128,256]{2,1,0:T(8,128)(2,1)}, u32[]{:S(2)}) copy-start(bf16[8,128,256]{2,1,0:T(8,128)(2,1)} %w_in.1) | copy-start | bytes 1572868
  3.6 0.8 %copy-start.2 = (bf16[1,1,128,128]{3,2,1,0:T(8,128)(2,1)S(1)}, bf16[1,1,128,128]{3,2,1,0:T(8,128)(2,1)}, u32[]{:S(2)}) copy-start(bf16[1,1,128,128]{3,2,1,0:T(8,128)(2,1)} %param.9) | copy-start | bytes 98308
  4.4 0.7 %copy-start.3 = (f32[8,256]{1,0:T(8,128)S(1)}, f32[8,256]{1,0:T(8,128)}, u32[]{:S(2)}) copy-start(f32[8,256]{1,0:T(8,128)} %b_in.1) | copy-start | bytes 24580
  5.0 0.7 %copy-start.4 = (f32[8,256]{1,0:T(8,128)S(1)}, f32[8,256]{1,0:T(8,128)}, u32[]{:S(2)}) copy-start(f32[8,256]{1,0:T(8,128)} %b_hid.1) | copy-start | bytes 24580
  5.7 0.7 %copy-start.5 = (bf16[8,2,256]{2,1,0:T(2,128)(2,1)S(1)}, bf16[8,2,256]{2,1,0:T(2,128)(2,1)}, u32[]{:S(2)}) copy-start(bf16[8,2,256]{2,1,0:T(2,128)(2,1)} %w_out.1) | copy-start | bytes 24580

commit v2 on v1

--- a/solution.py
+++ b/solution.py
@@ -38,19 +38,35 @@
     return value
 
 
-def slab_kernel(
-    desc_ref, pos_ref, species_ref, counts_ref, w_in, b_in, w_hid, b_hid, w_out, out_ref
-):
-    members = w_in.shape[0]
-    slots = desc_ref.shape[0]
-    species = species_ref[0]
-    slot_iota = lax.broadcasted_iota(jnp.int32, (1, slots), 1)
-    occupancy = (slot_iota < counts_ref[0, 0]).astype(jnp.float32)
-    widths = choose(species, (0.3, 0.4, 0.5, 0.35))
-    shifts = choose(species, (-0.8, 0.4, 1.2, -0.3))
+def slab_kernel(*refs):
+    sources, out_ref, landed, done = refs[:9], refs[9], refs[10:19], refs[19]
+    members = sources[4].shape[0]
+    copies = []
+
+    def fetch(source, target):
+        copy = pltpu.make_async_copy(source, target, done.at[len(copies)])
+        copy.start()
+        copies.append(copy)
+        return copy
+
+    desc_ref, pos_ref, species_ref, counts_ref, w_in, b_in, w_hid, b_hid, w_out = landed
+    early = [fetch(sources[k], landed[k]) for k in (0, 5)]
+    first_in = [fetch(sources[4].at[m], w_in.at[m]) for m in range(1)]
+    early.append(fetch(sources[7], b_hid))
+    hidden = [fetch(sources[6].at[m], w_hid.at[m]) for m in range(1)]
+    early.append(fetch(sources[8], w_out))
+    for m in range(1, members):
+        first_in.append(fetch(sources[4].at[m], w_in.at[m]))
+        hidden.append(fetch(sources[6].at[m], w_hid.at[m]))
+    late = [fetch(sources[k], landed[k]) for k in (1, 2, 3)]
+    for copy in early:
+        copy.wait()
     rows = desc_ref[...]
+    slots = rows.shape[0]
     electro, raw = [], []
     for m in range(members):
+        first_in[m].wait()
+        hidden[m].wait()
         first = jnp.tanh(
             jnp.dot(rows, w_in[m], preferred_element_type=jnp.float32) + b_in[m : m + 1, :]
         ).astype(jnp.bfloat16)
@@ -62,6 +78,13 @@
         )
         electro.append(outputs[0:1])
         raw.append(outputs[1:2])
+    for copy in late:
+        copy.wait()
+    species = species_ref[0]
+    slot_iota = lax.broadcasted_iota(jnp.int32, (1, slots), 1)
+    occupancy = (slot_iota < counts_ref[0, 0]).astype(jnp.float32)
+    widths = choose(species, (0.3, 0.4, 0.5, 0.35))
+    shifts = choose(species, (-0.8, 0.4, 1.2, -0.3))
     raw = jnp.concatenate(raw, axis=0)
     hardness = 2.5 + (jnp.maximum(raw, 0.0) + jnp.log1p(jnp.exp(-jnp.abs(raw))))
     right = -(jnp.concatenate(electro, axis=0) + shifts) * occupancy
@@ -136,25 +159,31 @@
             width = columns - abs(db)
 
             def line(a, carry, number=number, da=da, db=db, low_col=low_col, width=width):
+                pairs = []
                 for step in range(width):
                     c = a * columns + (low_col + step)
                     d = (a + da) * columns + (low_col + step + db)
-                    carry = handle(c, d, starts[number] + a * width + step, number == 0, carry)
-                return carry
+                    pairs.append((c, d, starts[number] + a * width + step))
+                return handle(pairs, number == 0, carry)
 
             yield line, rows - da
 
-    def first_pass(c, d, place, own, carry):
-        for first_row in range(0, slots, 32):
-            high, low = halves(pair_block(cols, slab_ref, c, d, first_row, 32, own))
-            k_high[place, first_row : first_row + 32, :] = high
-            k_low[place, first_row : first_row + 32, :] = low
-        high, low = k_high[place], k_low[place]
-        far = vecs[d]
-        sums[c] += times_t(far, high) + times_t(far, low)
-        if not own:
-            near = vecs[c]
-            sums[d] += times(near, high) + times(near, low)
+    def first_pass(pairs, own, carry):
+        terms = []
+        for c, d, place in pairs:
+            parts = []
+            for first_row in range(0, slots, 32):
+                parts.append(halves(pair_block(cols, slab_ref, c, d, first_row, 32, own)))
+            high, low = (jnp.concatenate(part, axis=0) for part in zip(*parts))
+            k_high[place] = high
+            k_low[place] = low
+            far = vecs[d]
+            terms.append((c, times_t(far, high) + times_t(far, low)))
+            if not own:
+                near = vecs[c]
+                terms.append((d, times(near, high) + times(near, low)))
+        for cell, term in terms:
+            sums[cell] += term
         return carry
 
     for line, length in each_pair(first_pass):
@@ -201,11 +230,14 @@
         prod1 += jnp.concatenate([hard, hard], axis=0) * square
         total1 += left
 
-    def second_pass(c, d, place, own, carry):
-        near = resid_half[c]
-        image = times(near, k_high[place]) + times(near, k_low[place])
-        part = (image[0:16] + image[16:32]) * resid[d]
-        return carry + (part if own else 2.0 * part)
+    def second_pass(pairs, own, carry):
+        parts = []
+        for c, d, place in pairs:
+            near = resid_half[c]
+            image = times(near, k_high[place]) + times(near, k_low[place])
+            parts.append((image[0:16] + image[16:32]) * resid[d])
+        total = sum(parts[1:], parts[0])
+        return carry + (total if own else 2.0 * total)
 
     for line, length in each_pair(second_pass):
         prod1 = lax.fori_loop(0, length, line, prod1)
@@ -222,23 +254,14 @@
     out_ref[...] = answer[0:members] - multiplier * answer[members:]
 
 
-def gathered(descriptors, positions, species, counts, w_in, b_in, w_hid, b_hid, w_out):
+def solve_only(slabs):
     rows, columns = lax.axis_size("cell"), lax.axis_size("sub")
-    cells, slots, members = rows * columns, descriptors.shape[2], w_in.shape[0]
+    cells, _, slots = slabs.shape
     vmem = pl.BlockSpec(memory_space=pltpu.VMEM)
-    slabs = pl.pallas_call(
-        slab_kernel,
-        out_shape=jax.ShapeDtypeStruct((cells, ROWS, slots), jnp.float32),
-        in_specs=[vmem] * 3 + [pl.BlockSpec(memory_space=pltpu.SMEM)] + [vmem] * 5,
-        out_specs=vmem,
-        compiler_params=pltpu.CompilerParams(vmem_limit_bytes=32 << 20),
-        name="slab",
-    )(descriptors.reshape(slots, -1), positions, species, counts, w_in, b_in, w_hid, b_hid, w_out)
-    slabs = lax.all_to_all(slabs, ("cell", "sub"), 0, 0, tiled=True)
     blocks = sum(pair_counts(rows, columns))
-    charges = pl.pallas_call(
+    return pl.pallas_call(
         lambda *refs: solve_kernel((rows, columns), *refs),
-        out_shape=jax.ShapeDtypeStruct((members, slots), jnp.float32),
+        out_shape=jax.ShapeDtypeStruct((HARD, slots), jnp.float32),
         in_specs=[vmem],
         out_specs=vmem,
         scratch_shapes=[
@@ -253,6 +276,29 @@
         compiler_params=pltpu.CompilerParams(vmem_limit_bytes=32 << 20),
         name="solve",
     )(slabs)
+
+
+def gathered(descriptors, positions, species, counts, w_in, b_in, w_hid, b_hid, w_out):
+    rows, columns = lax.axis_size("cell"), lax.axis_size("sub")
+    cells, slots, members = rows * columns, descriptors.shape[2], w_in.shape[0]
+    vmem = pl.BlockSpec(memory_space=pltpu.VMEM)
+    args = (
+        descriptors.reshape(slots, -1), positions, species, counts, w_in, b_in, w_hid, b_hid, w_out
+    )
+    landed = [
+        (pltpu.SMEM if arg is counts else pltpu.VMEM)(arg.shape, arg.dtype) for arg in args
+    ]
+    slabs = pl.pallas_call(
+        slab_kernel,
+        out_shape=jax.ShapeDtypeStruct((cells, ROWS, slots), jnp.float32),
+        in_specs=[pl.BlockSpec(memory_space=pltpu.HBM)] * len(args),
+        out_specs=vmem,
+        scratch_shapes=landed + [pltpu.SemaphoreType.DMA((7 + 2 * members,))],
+        compiler_params=pltpu.CompilerParams(vmem_limit_bytes=32 << 20),
+        name="slab",
+    )(*args)
+    slabs = lax.all_to_all(slabs, ("cell", "sub"), 0, 0, tiled=True)
+    charges = solve_only(slabs)
     return charges.reshape(members, 1, 1, slots)
 
 

time: 40.8 us -> 43.8 us (1.074)
  Pallas kernels: 17.8 us -> 20.7 us
    pallas_call x1, Pallas kernels: 2.21 us -> 5.68 us  [gathered(): pl.pallas_call(slab_kernel, out_shape=jax.ShapeDtypeStruct((cells, ROWS,...]
    pallas_call x1, Pallas kernels: 15.6 us -> 15 us  [solve_only(): pl.pallas_call(lambda *refs: solve_kernel((rows, columns), *refs), out_sh...]
where the time goes in v2:
time: 43.8 us; the launch traced here: 43.3 us
  Pallas kernels  20.7 us (47%)
  blocking collectives  16.2 us (37%)
  local copies, waits for them, and re-layouts  5.75 us (13%)
  between operations  0.7 us (2%)
    all_to_all x1, blocking collectives, gathered(): slabs = lax.all_to_all(slabs, ('cell', 'sub'), 0, 0, tiled=True)  16.2 us
    pallas_call x1, Pallas kernels, solve_only(): pl.pallas_call(lambda *refs: solve_kernel((rows, columns), *refs), out_sh...  15 us
    unnamed x16, local copies, waits for them, and re-layouts  5.75 us
    pallas_call x1, Pallas kernels, gathered(): pl.pallas_call(slab_kernel, out_shape=jax.ShapeDtypeStruct((cells, ROWS,...  5.68 us

profile of v2, /device:TPU:0, one launch (start us, length us, event | category | flops | bytes accessed | tf_op | source)
XLA Modules:
  0.0 43.3 jit_solution(6133712510915535072)
XLA Ops:
  0.0 0.0 copy-start.6
  0.7 0.0 copy-start.7
  0.7 0.0 copy-done.6
  0.7 0.6 %copy-done.7 = s32[1,1,128]{2,1,0:T(1,128)S(1)} copy-done((s32[1,1,128]{2,1,0:T(1,128)S(1)}, s32[1,1,128]{2,1,0:T(1,128)}, u32[]{:S(2)}) %copy-start.7) | copy-done | bytes 536
  1.3 0.0 copy-start
  1.3 1.2 %copy-done = bf16[8,256,256]{2,1,0:T(8,128)(2,1)S(1)} copy-done((bf16[8,256,256]{2,1,0:T(8,128)(2,1)S(1)}, bf16[8,256,256]{2,1,0:T(8,128)(2,1)}, u32[]{:S(2)}) %copy-start) | copy-done | bytes 1048600
  2.6 0.0 copy-start.1
  2.6 1.0 %copy-done.1 = bf16[8,128,256]{2,1,0:T(8,128)(2,1)S(1)} copy-done((bf16[8,128,256]{2,1,0:T(8,128)(2,1)S(1)}, bf16[8,128,256]{2,1,0:T(8,128)(2,1)}, u32[]{:S(2)}) %copy-start.1) | copy-done | bytes 524312
  3.6 0.0 copy-start.2
  3.6 0.8 %copy-done.2 = bf16[1,1,128,128]{3,2,1,0:T(8,128)(2,1)S(1)} copy-done((bf16[1,1,128,128]{3,2,1,0:T(8,128)(2,1)S(1)}, bf16[1,1,128,128]{3,2,1,0:T(8,128)(2,1)}, u32[]{:S(2)}) %copy-start.2) | copy-done | bytes 32792
  4.4 0.0 copy-start.3
  4.4 0.7 %copy-done.3 = f32[8,256]{1,0:T(8,128)S(1)} copy-done((f32[8,256]{1,0:T(8,128)S(1)}, f32[8,256]{1,0:T(8,128)}, u32[]{:S(2)}) %copy-start.3) | copy-done | bytes 8216
  5.0 0.0 copy-start.4
  5.1 0.7 %copy-done.4 = f32[8,256]{1,0:T(8,128)S(1)} copy-done((f32[8,256]{1,0:T(8,128)S(1)}, f32[8,256]{1,0:T(8,128)}, u32[]{:S(2)}) %copy-start.4) | copy-done | bytes 8216
  5.7 0.0 copy-start.5
  5.7 0.7 %copy-done.5 = bf16[8,2,256]{2,1,0:T(2,128)(2,1)S(1)} copy-done((bf16[8,2,256]{2,1,0:T(2,128)(2,1)S(1)}, bf16[8,2,256]{2,1,0:T(2,128)(2,1)}, u32[]{:S(2)}) %copy-start.5) | copy-done | bytes 8216
  6.4 5.7 %slab.1 = f32[16,24,128]{2,1,0:T(8,128)S(1)} custom-call(bf16[128,128]{1,0:T(8,128)(2,1)S(1)} %bitcast.4, f32[3,1,1,128]{3,2,1,0:T(1,128)S(1)} %copy-done.6, s32[1,1,128]{2,1,0:T(1,128)S(1)} %copy-done.7, s32[1,1]{1,0:T(1,128)S(6)} %copy.11.refs_3_, bf16[8,128,256]{2,1,0:T(8,128)(2,1)S(1)} %copy-done.1, f32[8,256]{1,0:T(8,128)S(1)} %copy-done.3, ...), custom_call_target="tpu_custom_call" | custom-call | tf_op jit(solution)/shard_map/slab/pallas_call | solution.py:291
  12.1 16.2 %all_to_all.5.refs_0_ = f32[16,24,128]{2,1,0:T(8,128)S(1)} all-to-all(f32[16,24,128]{2,1,0:T(8,128)S(1)} %slab.1), channel_id=1, replica_groups=mesh['rep'=2,'cell'=4,'sub'=4] {'cell','sub'}, dimensions={0} | all-to-all | bytes 393216 | tf_op jit(solution)/shard_map/all_to_all | solution.py:300
  28.3 15.0 %solve.1 = f32[8,128]{1,0:T(8,128)} custom-call(f32[16,24,128]{2,1,0:T(8,128)S(1)} %all_to_all.5.refs_0_), custom_call_target="tpu_custom_call" | custom-call | tf_op jit(solution)/shard_map/solve/pallas_call | solution.py:262
Async XLA Ops:
  0.0 0.7 %copy-start.6 = (f32[3,1,1,128]{3,2,1,0:T(1,128)S(1)}, f32[3,1,1,128]{3,2,1,0:T(1,128)}, u32[]{:S(2)}) copy-start(f32[3,1,1,128]{3,2,1,0:T(1,128)} %refs_1_.1) | copy-start | bytes 4612
  0.7 0.7 %copy-start.7 = (s32[1,1,128]{2,1,0:T(1,128)S(1)}, s32[1,1,128]{2,1,0:T(1,128)}, u32[]{:S(2)}) copy-start(s32[1,1,128]{2,1,0:T(1,128)} %refs_2_.1) | copy-start | bytes 1540
  1.3 1.2 %copy-start = (bf16[8,256,256]{2,1,0:T(8,128)(2,1)S(1)}, bf16[8,256,256]{2,1,0:T(8,128)(2,1)}, u32[]{:S(2)}) copy-start(bf16[8,256,256]{2,1,0:T(8,128)(2,1)} %refs_6_.1) | copy-start | bytes 3145732
  2.6 1.0 %copy-start.1 = (bf16[8,128,256]{2,1,0:T(8,128)(2,1)S(1)}, bf16[8,128,256]{2,1,0:T(8,128)(2,1)}, u32[]{:S(2)}) copy-start(bf16[8,128,256]{2,1,0:T(8,128)(2,1)} %refs_4_.1) | copy-start | bytes 1572868
  3.6 0.8 %copy-start.2 = (bf16[1,1,128,128]{3,2,1,0:T(8,128)(2,1)S(1)}, bf16[1,1,128,128]{3,2,1,0:T(8,128)(2,1)}, u32[]{:S(2)}) copy-start(bf16[1,1,128,128]{3,2,1,0:T(8,128)(2,1)} %param.9) | copy-start | bytes 98308
  4.4 0.7 %copy-start.3 = (f32[8,256]{1,0:T(8,128)S(1)}, f32[8,256]{1,0:T(8,128)}, u32[]{:S(2)}) copy-start(f32[8,256]{1,0:T(8,128)} %refs_5_.1) | copy-start | bytes 24580
  5.0 0.7 %copy-start.4 = (f32[8,256]{1,0:T(8,128)S(1)}, f32[8,256]{1,0:T(8,128)}, u32[]{:S(2)}) copy-start(f32[8,256]{1,0:T(8,128)} %refs_7_.1) | copy-start | bytes 24580
  5.7 0.7 %copy-start.5 = (bf16[8,2,256]{2,1,0:T(2,128)(2,1)S(1)}, bf16[8,2,256]{2,1,0:T(2,128)(2,1)}, u32[]{:S(2)}) copy-start(bf16[8,2,256]{2,1,0:T(2,128)(2,1)} %refs_8_.1) | copy-start | bytes 24580

commit v3 on v2

--- a/solution.py
+++ b/solution.py
@@ -294,7 +294,7 @@
         in_specs=[pl.BlockSpec(memory_space=pltpu.HBM)] * len(args),
         out_specs=vmem,
         scratch_shapes=landed + [pltpu.SemaphoreType.DMA((7 + 2 * members,))],
-        compiler_params=pltpu.CompilerParams(vmem_limit_bytes=32 << 20),
+        compiler_params=pltpu.CompilerParams(vmem_limit_bytes=60 << 20),
         name="slab",
     )(*args)
     slabs = lax.all_to_all(slabs, ("cell", "sub"), 0, 0, tiled=True)

time: 43.8 us -> 37.6 us (0.86)
  local copies, waits for them, and re-layouts: 5.75 us -> 0 us
    unnamed x16 -> x0, local copies, waits for them, and re-layouts: 5.75 us -> none
where the time goes in v3:
time: 37.6 us; the launch traced here: 37.3 us
  Pallas kernels  20.3 us (54%)
  blocking collectives  16.4 us (44%)
  between operations  0.66 us (2%)
    all_to_all x1, blocking collectives, gathered(): slabs = lax.all_to_all(slabs, ('cell', 'sub'), 0, 0, tiled=True)  16.4 us
    pallas_call x1, Pallas kernels, solve_only(): pl.pallas_call(lambda *refs: solve_kernel((rows, columns), *refs), out_sh...  15 us
    pallas_call x1, Pallas kernels, gathered(): pl.pallas_call(slab_kernel, out_shape=jax.ShapeDtypeStruct((cells, ROWS,...  5.25 us

profile of v3, /device:TPU:0, one launch (start us, length us, event | category | flops | bytes accessed | tf_op | source)
XLA Modules:
  0.0 37.3 jit_solution(13693946596659242524)
XLA Ops:
  0.7 5.3 %slab.1 = f32[16,24,128]{2,1,0:T(8,128)} custom-call(bf16[128,128]{1,0:T(8,128)(2,1)} %bitcast.4, f32[3,1,1,128]{3,2,1,0:T(1,128)} %refs_1_.1, s32[1,1,128]{2,1,0:T(1,128)} %refs_2_.1, s32[1,1]{1,0:T(1,128)S(6)} %copy.11.refs_3_, bf16[8,128,256]{2,1,0:T(8,128)(2,1)} %refs_4_.1, f32[8,256]{1,0:T(8,128)} %refs_5_.1, bf16[8,256,256]{2,1,0:T(8,128)(2,1)} %refs_6_.1, ...), custom_call_target="tpu_custom_call" | custom-call | tf_op jit(solution)/shard_map/slab/pallas_call | solution.py:291
  5.9 16.4 %all_to_all.5.refs_0_ = f32[16,24,128]{2,1,0:T(8,128)S(1)} all-to-all(f32[16,24,128]{2,1,0:T(8,128)} %slab.1), channel_id=1, replica_groups=mesh['rep'=2,'cell'=4,'sub'=4] {'cell','sub'}, dimensions={0} | all-to-all | bytes 393216 | tf_op jit(solution)/shard_map/all_to_all | solution.py:300
  22.3 15.0 %solve.1 = f32[8,128]{1,0:T(8,128)} custom-call(f32[16,24,128]{2,1,0:T(8,128)S(1)} %all_to_all.5.refs_0_), custom_call_target="tpu_custom_call" | custom-call | tf_op jit(solution)/shard_map/solve/pallas_call | solution.py:262

commit v4 on v3

--- a/solution.py
+++ b/solution.py
@@ -22,9 +22,13 @@
     1.4031096882113396e-09,
 )
 
-HARD, PLACE, SPREAD, FULL, ROWS = 8, 16, 19, 20, 24
+WIDTHS = (0.3, 0.4, 0.5, 0.35)
+
+HARD, PLACE, KIND, FULL, ROWS = 8, 16, 19, 20, 24
+SQUARE, FEATURES = 24, 48
 OFFSETS = ((0, 0), (0, 1), (1, -1), (1, 0), (1, 1))
 MOST_BLOCKS = 128
+CHUNK = 128
 
 
 def pair_counts(rows, cols):
@@ -83,13 +87,12 @@
     species = species_ref[0]
     slot_iota = lax.broadcasted_iota(jnp.int32, (1, slots), 1)
     occupancy = (slot_iota < counts_ref[0, 0]).astype(jnp.float32)
-    widths = choose(species, (0.3, 0.4, 0.5, 0.35))
     shifts = choose(species, (-0.8, 0.4, 1.2, -0.3))
     raw = jnp.concatenate(raw, axis=0)
     hardness = 2.5 + (jnp.maximum(raw, 0.0) + jnp.log1p(jnp.exp(-jnp.abs(raw))))
     right = -(jnp.concatenate(electro, axis=0) + shifts) * occupancy
     atoms = jnp.concatenate(
-        [pos_ref[0, 0], pos_ref[1, 0], pos_ref[2, 0], widths * widths, occupancy]
+        [pos_ref[0, 0], pos_ref[1, 0], pos_ref[2, 0], species.astype(jnp.float32), occupancy]
         + [jnp.zeros((1, slots), jnp.float32)] * (ROWS - FULL - 1),
         axis=0,
     )
@@ -99,16 +102,39 @@
         out_ref[peer, PLACE:ROWS, :] = atoms
 
 
-def pair_block(cols, slab_ref, c, d, first_row, height, own):
-    span = pl.ds(first_row, height)
-
-    def gap(k):
-        return cols[c, span, k : k + 1] - slab_ref[d, PLACE + k : PLACE + k + 1, :]
-
-    da, db, dc = gap(0), gap(1), gap(2)
-    capped = jnp.minimum(da * da + db * db + dc * dc, 1.0)
+def thirds(values):
+    high = values.astype(jnp.bfloat16).astype(jnp.float32)
+    rest = values - high
+    middle = rest.astype(jnp.bfloat16).astype(jnp.float32)
+    return high, middle, rest - middle
+
+
+def pair_features(places, kind):
+    one, zero = jnp.ones_like(kind), jnp.zeros_like(kind)
+    near, far = [], []
+    for place in places:
+        h, m, l = thirds(place)
+        near += [h, h, m, m, h, l]
+        far += [-2.0 * v for v in (h, m, h, m, l, h)]
+    norm = list(thirds(sum(place * place for place in places)))
+    near += norm + [one] * 3
+    far += [one] * 3 + norm
+    count = len(WIDTHS)
+    near += [(kind == k).astype(jnp.float32) for k in range(count)] * 3
+    pairs = [
+        choose(kind, [(WIDTHS[k] ** 2 + other**2) ** -0.5 for other in WIDTHS])
+        for k in range(count)
+    ]
+    far += [part for third in zip(*map(thirds, pairs)) for part in third]
+    rest = [zero] * (FEATURES - len(near))
+    return near + rest, far + rest
+
+
+def pair_block(products, first_row, own):
+    slots = products.shape[1] // 2
+    capped = jnp.minimum(products[:, 0:slots], 1.0)
+    inv = products[:, slots:]
     left = 1.0 - capped
-    inv = lax.rsqrt(cols[c, span, 3:4] + slab_ref[d, SPREAD : SPREAD + 1, :])
     y = (capped + 1e-06) * (inv * inv) - ERF_CENTRE
     value = jnp.full_like(y, 0.005 * ERF_SERIES[-1])
     for term in ERF_SERIES[-2::-1]:
@@ -136,58 +162,68 @@
     return high, (values - high.astype(jnp.float32)).astype(jnp.bfloat16)
 
 
-def solve_kernel(grid, slab_ref, out_ref, cols, vecs, sums, resid, resid_half, k_high, k_low):
+def solve_kernel(grid, slab_ref, out_ref, feats, near, far, vecs, sums, resid, resid_half, blocks):
     rows, columns = grid
     cells, _, slots = slab_ref.shape
     members = HARD
-    starts = [0]
-    for count in pair_counts(rows, columns):
-        starts.append(starts[-1] + count)
-
+
+    centres = (rows / 2, columns / 2, 0.5)
+    rows_of = pair_features(
+        [slab_ref[:, PLACE + k, :] - centres[k] for k in range(3)], slab_ref[:, KIND, :]
+    )
+    for k, row in enumerate(rows_of[0] + rows_of[1]):
+        feats[:, k, :] = row
+    blank = jnp.zeros((SQUARE, slots), jnp.float32)
     for c in range(cells):
-        cols[c] = slab_ref[c, PLACE:ROWS, :].T
+        near[c] = feats[c, 0:FEATURES, :].T.astype(jnp.bfloat16)
+        apart = jnp.concatenate([feats[c, FEATURES : FEATURES + SQUARE, :], blank], axis=0)
+        spread = jnp.concatenate([blank, feats[c, FEATURES + SQUARE :, :]], axis=0)
+        far[c] = jnp.concatenate([apart, spread], axis=1).astype(jnp.bfloat16)
         high, low = halves(slab_ref[c, 0:HARD, :])
-        vecs[c, 0:16, :] = jnp.concatenate([high.astype(jnp.float32), low.astype(jnp.float32)], axis=0).astype(jnp.bfloat16)
         full = slab_ref[c, FULL : FULL + 1, :]
         row = lax.broadcasted_iota(jnp.int32, (16, slots), 0)
-        vecs[c, 16:32, :] = jnp.where(row == 0, full, 0.0).astype(jnp.bfloat16)
+        lines = [high.astype(jnp.float32), low.astype(jnp.float32), jnp.where(row == 0, full, 0.0)]
+        lines = jnp.concatenate(lines, axis=0).astype(jnp.bfloat16)
+        vecs[c] = jnp.concatenate([lines, lines], axis=1)
         sums[c] = jnp.zeros_like(sums[c])
 
-    def each_pair(handle):
-        for number, (da, db) in enumerate(OFFSETS):
-            low_col = max(0, -db)
-            width = columns - abs(db)
-
-            def line(a, carry, number=number, da=da, db=db, low_col=low_col, width=width):
-                pairs = []
-                for step in range(width):
-                    c = a * columns + (low_col + step)
-                    d = (a + da) * columns + (low_col + step + db)
-                    pairs.append((c, d, starts[number] + a * width + step))
-                return handle(pairs, number == 0, carry)
-
-            yield line, rows - da
-
-    def first_pass(pairs, own, carry):
+    def row_pairs(a, last):
+        pairs = []
+        for da, db in OFFSETS[:2] if last else OFFSETS:
+            for column in range(max(0, -db), columns - max(0, db)):
+                c = a * columns + column
+                place = a * (5 * columns - 3) + len(pairs)
+                pairs.append((c, c + da * columns + db, place, da == db == 0))
+        return pairs
+
+    def over_rows(handle, carry):
+        for a in range(rows):
+            carry = handle(row_pairs(a, a == rows - 1), carry)
+        return carry
+
+    def build(pairs, carry):
+        for c, d, place, own in pairs:
+            for first_row in range(0, slots, CHUNK):
+                products = times(near[c, first_row : first_row + CHUNK, :], far[d])
+                high, low = halves(pair_block(products, first_row, own))
+                blocks[place, first_row : first_row + CHUNK, :] = high
+                blocks[place, slots + first_row : slots + first_row + CHUNK, :] = low
+        return carry
+
+    def first_pass(pairs, carry):
         terms = []
-        for c, d, place in pairs:
-            parts = []
-            for first_row in range(0, slots, 32):
-                parts.append(halves(pair_block(cols, slab_ref, c, d, first_row, 32, own)))
-            high, low = (jnp.concatenate(part, axis=0) for part in zip(*parts))
-            k_high[place] = high
-            k_low[place] = low
-            far = vecs[d]
-            terms.append((c, times_t(far, high) + times_t(far, low)))
+        for c, d, place, own in pairs:
+            block = blocks[place]
+            terms.append((d, times(vecs[c], block)))
             if not own:
-                near = vecs[c]
-                terms.append((d, times(near, high) + times(near, low)))
+                image = times_t(vecs[d, :, 0:slots], block)
+                terms.append((c, image[:, 0:slots] + image[:, slots:]))
         for cell, term in terms:
             sums[cell] += term
         return carry
 
-    for line, length in each_pair(first_pass):
-        lax.fori_loop(0, length, line, 0)
+    over_rows(build, 0)
+    over_rows(first_pass, 0)
 
     def applied(c):
         hard = slab_ref[c, HARD:PLACE, :]
@@ -223,24 +259,21 @@
         left = both(right, full) - alpha0 * jnp.concatenate([image_s, image_u], axis=0)
         resid[c] = left
         high, low = halves(left)
-        resid_half[c, 0:16, :] = high
-        resid_half[c, 16:32, :] = low
+        lines = jnp.concatenate([high, low], axis=0)
+        resid_half[c] = jnp.concatenate([lines, lines], axis=1)
         square = left * left
         norm1 += square
         prod1 += jnp.concatenate([hard, hard], axis=0) * square
         total1 += left
 
-    def second_pass(pairs, own, carry):
-        parts = []
-        for c, d, place in pairs:
-            near = resid_half[c]
-            image = times(near, k_high[place]) + times(near, k_low[place])
-            parts.append((image[0:16] + image[16:32]) * resid[d])
-        total = sum(parts[1:], parts[0])
-        return carry + (total if own else 2.0 * total)
-
-    for line, length in each_pair(second_pass):
-        prod1 = lax.fori_loop(0, length, line, prod1)
+    def second_pass(pairs, carry):
+        for c, d, place, own in pairs:
+            image = times(resid_half[c], blocks[place])
+            part = (image[0:16] + image[16:32]) * resid[d]
+            carry = carry + (part if own else 2.0 * part)
+        return carry
+
+    prod1 = over_rows(second_pass, prod1)
 
     norm1, prod1, total1 = over(norm1), over(prod1), over(total1)
     momentum = norm1 / norm0
@@ -265,13 +298,14 @@
         in_specs=[vmem],
         out_specs=vmem,
         scratch_shapes=[
-            pltpu.VMEM((cells, slots, ROWS - PLACE), jnp.float32),
-            pltpu.VMEM((cells, 32, slots), jnp.bfloat16),
+            pltpu.VMEM((cells, 2 * FEATURES, slots), jnp.float32),
+            pltpu.VMEM((cells, slots, FEATURES), jnp.bfloat16),
+            pltpu.VMEM((cells, FEATURES, 2 * slots), jnp.bfloat16),
+            pltpu.VMEM((cells, 32, 2 * slots), jnp.bfloat16),
             pltpu.VMEM((cells, 32, slots), jnp.float32),
             pltpu.VMEM((cells, 16, slots), jnp.float32),
-            pltpu.VMEM((cells, 32, slots), jnp.bfloat16),
-            pltpu.VMEM((blocks, slots, slots), jnp.bfloat16),
-            pltpu.VMEM((blocks, slots, slots), jnp.bfloat16),
+            pltpu.VMEM((cells, 32, 2 * slots), jnp.bfloat16),
+            pltpu.VMEM((blocks, 2 * slots, slots), jnp.bfloat16),
         ],
         compiler_params=pltpu.CompilerParams(vmem_limit_bytes=32 << 20),
         name="solve",

time: 37.6 us -> 31 us (0.82)
  Pallas kernels: 20.3 us -> 13.8 us
    pallas_call x1, Pallas kernels: 15 us -> 8.51 us  [solve_only(): pl.pallas_call(lambda *refs: solve_kernel((rows, columns), *refs), out_sh...]
where the time goes in v4:
time: 31 us; the launch traced here: 30.8 us
  blocking collectives  16.4 us (53%)
  Pallas kernels  13.8 us (45%)
  between operations  0.66 us (2%)
    all_to_all x1, blocking collectives, gathered(): slabs = lax.all_to_all(slabs, ('cell', 'sub'), 0, 0, tiled=True)  16.4 us
    pallas_call x1, Pallas kernels, solve_only(): pl.pallas_call(lambda *refs: solve_kernel((rows, columns), *refs), out_sh...  8.51 us
    pallas_call x1, Pallas kernels, gathered(): pl.pallas_call(slab_kernel, out_shape=jax.ShapeDtypeStruct((cells, ROWS,...  5.25 us

profile of v4, /device:TPU:0, one launch (start us, length us, event | category | flops | bytes accessed | tf_op | source)
XLA Modules:
  0.0 30.8 jit_solution(13295883772915661623)
XLA Ops:
  0.7 5.3 %slab.1 = f32[16,24,128]{2,1,0:T(8,128)} custom-call(bf16[128,128]{1,0:T(8,128)(2,1)} %bitcast.4, f32[3,1,1,128]{3,2,1,0:T(1,128)} %refs_1_.1, s32[1,1,128]{2,1,0:T(1,128)} %refs_2_.1, s32[1,1]{1,0:T(1,128)S(6)} %copy.11.refs_3_, bf16[8,128,256]{2,1,0:T(8,128)(2,1)} %refs_4_.1, f32[8,256]{1,0:T(8,128)} %refs_5_.1, bf16[8,256,256]{2,1,0:T(8,128)(2,1)} %refs_6_.1, ...), custom_call_target="tpu_custom_call" | custom-call | tf_op jit(solution)/shard_map/slab/pallas_call | solution.py:325
  5.9 16.4 %all_to_all.5.refs_0_ = f32[16,24,128]{2,1,0:T(8,128)S(1)} all-to-all(f32[16,24,128]{2,1,0:T(8,128)} %slab.1), channel_id=1, replica_groups=mesh['rep'=2,'cell'=4,'sub'=4] {'cell','sub'}, dimensions={0} | all-to-all | bytes 393216 | tf_op jit(solution)/shard_map/all_to_all | solution.py:334
  22.3 8.5 %solve.1 = f32[8,128]{1,0:T(8,128)} custom-call(f32[16,24,128]{2,1,0:T(8,128)S(1)} %all_to_all.5.refs_0_), custom_call_target="tpu_custom_call" | custom-call | tf_op jit(solution)/shard_map/solve/pallas_call | solution.py:295

commit v5 on v4

--- a/solution.py
+++ b/solution.py
@@ -7,19 +7,16 @@
 
 ITERS = 2
 
-ERF_CENTRE = 1.000001 / 0.36
 ERF_SERIES = (
-    0.5889464636197189,
-    -0.09338177281045029,
-    0.018898799573350084,
-    -0.003564793815999453,
-    0.0005967292996019212,
-    -8.816834134949323e-05,
-    1.1544704937919275e-05,
-    -1.3330679803919568e-06,
-    1.4072010724176845e-07,
-    -1.592848428884591e-08,
-    1.4031096882113396e-09,
+    1.1283791338788207,
+    -0.37612471240078243,
+    0.11282450088960652,
+    -0.026825992168818515,
+    0.005164800720113156,
+    -0.0008061635856414364,
+    9.67168369375208e-05,
+    -7.756955478859171e-06,
+    3.007955257374649e-07,
 )
 
 WIDTHS = (0.3, 0.4, 0.5, 0.35)
@@ -29,6 +26,8 @@
 OFFSETS = ((0, 0), (0, 1), (1, -1), (1, 0), (1, 1))
 MOST_BLOCKS = 128
 CHUNK = 128
+LAG = 12
+GROUP = 8
 
 
 def pair_counts(rows, cols):
@@ -54,34 +53,34 @@
         return copy
 
     desc_ref, pos_ref, species_ref, counts_ref, w_in, b_in, w_hid, b_hid, w_out = landed
-    early = [fetch(sources[k], landed[k]) for k in (0, 5)]
-    first_in = [fetch(sources[4].at[m], w_in.at[m]) for m in range(1)]
-    early.append(fetch(sources[7], b_hid))
-    hidden = [fetch(sources[6].at[m], w_hid.at[m]) for m in range(1)]
-    early.append(fetch(sources[8], w_out))
-    for m in range(1, members):
-        first_in.append(fetch(sources[4].at[m], w_in.at[m]))
-        hidden.append(fetch(sources[6].at[m], w_hid.at[m]))
+    early = [fetch(sources[k], landed[k]) for k in (0, 5, 4)]
+    middle = [fetch(sources[k], landed[k]) for k in (6, 7, 8)]
     late = [fetch(sources[k], landed[k]) for k in (1, 2, 3)]
     for copy in early:
         copy.wait()
     rows = desc_ref[...]
     slots = rows.shape[0]
-    electro, raw = [], []
+    firsts, electro, raw = [], [], []
     for m in range(members):
-        first_in[m].wait()
-        hidden[m].wait()
-        first = jnp.tanh(
-            jnp.dot(rows, w_in[m], preferred_element_type=jnp.float32) + b_in[m : m + 1, :]
-        ).astype(jnp.bfloat16)
-        second = jnp.tanh(
-            jnp.dot(first, w_hid[m], preferred_element_type=jnp.float32) + b_hid[m : m + 1, :]
-        ).astype(jnp.bfloat16)
-        outputs = lax.dot_general(
-            w_out[m], second, (((1,), (1,)), ((), ())), preferred_element_type=jnp.float32
-        )
-        electro.append(outputs[0:1])
-        raw.append(outputs[1:2])
+        summed = jnp.dot(rows, w_in[m], preferred_element_type=jnp.float32) + b_in[m : m + 1, :]
+        firsts.append(jnp.tanh(summed).astype(jnp.bfloat16))
+    for copy in middle:
+        copy.wait()
+    for start in range(0, members, GROUP):
+        group = range(start, start + GROUP)
+        seconds = []
+        for m in group:
+            summed = jnp.dot(firsts[m], w_hid[m], preferred_element_type=jnp.float32)
+            seconds.append(jnp.tanh(summed + b_hid[m : m + 1, :]).astype(jnp.bfloat16))
+        for m in group:
+            outputs = lax.dot_general(
+                w_out[m],
+                seconds[m - start],
+                (((1,), (1,)), ((), ())),
+                preferred_element_type=jnp.float32,
+            )
+            electro.append(outputs[0:1])
+            raw.append(outputs[1:2])
     for copy in late:
         copy.wait()
     species = species_ref[0]
@@ -115,10 +114,10 @@
     for place in places:
         h, m, l = thirds(place)
         near += [h, h, m, m, h, l]
-        far += [-2.0 * v for v in (h, m, h, m, l, h)]
-    norm = list(thirds(sum(place * place for place in places)))
-    near += norm + [one] * 3
-    far += [one] * 3 + norm
+        far += [2.0 * v for v in (h, m, h, m, l, h)]
+    norm = sum(place * place for place in places)
+    near += [*thirds(norm), one, one, one]
+    far += [-one, -one, -one, *thirds(1.0 - norm)]
     count = len(WIDTHS)
     near += [(kind == k).astype(jnp.float32) for k in range(count)] * 3
     pairs = [
@@ -132,10 +131,9 @@
 
 def pair_block(products, first_row, own):
     slots = products.shape[1] // 2
-    capped = jnp.minimum(products[:, 0:slots], 1.0)
+    left = jnp.maximum(products[:, 0:slots], 0.0)
     inv = products[:, slots:]
-    left = 1.0 - capped
-    y = (capped + 1e-06) * (inv * inv) - ERF_CENTRE
+    y = (1.000001 - left) * (inv * inv)
     value = jnp.full_like(y, 0.005 * ERF_SERIES[-1])
     for term in ERF_SERIES[-2::-1]:
         value = value * y + 0.005 * term
@@ -222,8 +220,11 @@
             sums[cell] += term
         return carry
 
-    over_rows(build, 0)
-    over_rows(first_pass, 0)
+    every = over_rows(lambda pairs, kept: kept + pairs, [])
+    for i in range(len(every) + LAG):
+        if i >= LAG:
+            first_pass(every[i - LAG : i - LAG + 1], 0)
+        build(every[i : i + 1], 0)
 
     def applied(c):
         hard = slab_ref[c, HARD:PLACE, :]
@@ -327,7 +328,7 @@
         out_shape=jax.ShapeDtypeStruct((cells, ROWS, slots), jnp.float32),
         in_specs=[pl.BlockSpec(memory_space=pltpu.HBM)] * len(args),
         out_specs=vmem,
-        scratch_shapes=landed + [pltpu.SemaphoreType.DMA((7 + 2 * members,))],
+        scratch_shapes=landed + [pltpu.SemaphoreType.DMA((len(args),))],
         compiler_params=pltpu.CompilerParams(vmem_limit_bytes=60 << 20),
         name="slab",
     )(*args)

time: 31 us -> 26.2 us (0.85)
  Pallas kernels: 13.8 us -> 8.93 us
    pallas_call x1, Pallas kernels: 5.25 us -> 2.66 us  [gathered(): pl.pallas_call(slab_kernel, out_shape=jax.ShapeDtypeStruct((cells, ROWS,...]
    pallas_call x1, Pallas kernels: 8.51 us -> 6.28 us  [solve_only(): pl.pallas_call(lambda *refs: solve_kernel((rows, columns), *refs), out_sh...]
where the time goes in v5:
time: 26.2 us; the launch traced here: 26 us
  blocking collectives  16.4 us (63%)
  Pallas kernels  8.93 us (34%)
  between operations  0.66 us (3%)
    all_to_all x1, blocking collectives, gathered(): slabs = lax.all_to_all(slabs, ('cell', 'sub'), 0, 0, tiled=True)  16.4 us
    pallas_call x1, Pallas kernels, solve_only(): pl.pallas_call(lambda *refs: solve_kernel((rows, columns), *refs), out_sh...  6.28 us
    pallas_call x1, Pallas kernels, gathered(): pl.pallas_call(slab_kernel, out_shape=jax.ShapeDtypeStruct((cells, ROWS,...  2.66 us

profile of v5, /device:TPU:0, one launch (start us, length us, event | category | flops | bytes accessed | tf_op | source)
XLA Modules:
  0.0 26.0 jit_solution(17512366556558213443)
XLA Ops:
  0.7 2.7 %slab.1 = f32[16,24,128]{2,1,0:T(8,128)} custom-call(bf16[128,128]{1,0:T(8,128)(2,1)} %bitcast.4, f32[3,1,1,128]{3,2,1,0:T(1,128)} %refs_1_.1, s32[1,1,128]{2,1,0:T(1,128)} %refs_2_.1, s32[1,1]{1,0:T(1,128)S(6)} %copy.11.refs_3_, bf16[8,128,256]{2,1,0:T(8,128)(2,1)} %refs_4_.1, f32[8,256]{1,0:T(8,128)} %refs_5_.1, bf16[8,256,256]{2,1,0:T(8,128)(2,1)} %refs_6_.1, ...), custom_call_target="tpu_custom_call" | custom-call | tf_op jit(solution)/shard_map/slab/pallas_call | solution.py:326
  3.3 16.4 %all_to_all.5.refs_0_ = f32[16,24,128]{2,1,0:T(8,128)S(1)} all-to-all(f32[16,24,128]{2,1,0:T(8,128)} %slab.1), channel_id=1, replica_groups=mesh['rep'=2,'cell'=4,'sub'=4] {'cell','sub'}, dimensions={0} | all-to-all | bytes 393216 | tf_op jit(solution)/shard_map/all_to_all | solution.py:335
  19.7 6.3 %solve.1 = f32[8,128]{1,0:T(8,128)} custom-call(f32[16,24,128]{2,1,0:T(8,128)S(1)} %all_to_all.5.refs_0_), custom_call_target="tpu_custom_call" | custom-call | tf_op jit(solution)/shard_map/solve/pallas_call | solution.py:296

commit v6 on v5

--- a/solution.py
+++ b/solution.py
@@ -28,6 +28,7 @@
 CHUNK = 128
 LAG = 12
 GROUP = 8
+SIDES = 2
 
 
 def pair_counts(rows, cols):
@@ -160,11 +161,16 @@
     return high, (values - high.astype(jnp.float32)).astype(jnp.bfloat16)
 
 
-def solve_kernel(grid, slab_ref, out_ref, feats, near, far, vecs, sums, resid, resid_half, blocks):
+def solve_kernel(
+    grid, mine_ref, theirs_ref, out_ref, slab_ref, feats, near, far, vecs, sums, resid, resid_half, blocks
+):
     rows, columns = grid
     cells, _, slots = slab_ref.shape
     members = HARD
-
+    side = lax.rem(lax.axis_index("sub"), SIDES)
+    for k in range(cells // SIDES):
+        slab_ref[SIDES * k + side] = mine_ref[k]
+        slab_ref[SIDES * k + (1 - side)] = theirs_ref[k]
     centres = (rows / 2, columns / 2, 0.5)
     rows_of = pair_features(
         [slab_ref[:, PLACE + k, :] - centres[k] for k in range(3)], slab_ref[:, KIND, :]
@@ -288,17 +294,18 @@
     out_ref[...] = answer[0:members] - multiplier * answer[members:]
 
 
-def solve_only(slabs):
+def solve_only(mine, theirs):
     rows, columns = lax.axis_size("cell"), lax.axis_size("sub")
-    cells, _, slots = slabs.shape
+    cells, slots = rows * columns, mine.shape[2]
     vmem = pl.BlockSpec(memory_space=pltpu.VMEM)
     blocks = sum(pair_counts(rows, columns))
     return pl.pallas_call(
         lambda *refs: solve_kernel((rows, columns), *refs),
         out_shape=jax.ShapeDtypeStruct((HARD, slots), jnp.float32),
-        in_specs=[vmem],
+        in_specs=[vmem] * SIDES,
         out_specs=vmem,
         scratch_shapes=[
+            pltpu.VMEM((cells, ROWS, slots), jnp.float32),
             pltpu.VMEM((cells, 2 * FEATURES, slots), jnp.float32),
             pltpu.VMEM((cells, slots, FEATURES), jnp.bfloat16),
             pltpu.VMEM((cells, FEATURES, 2 * slots), jnp.bfloat16),
@@ -310,7 +317,7 @@
         ],
         compiler_params=pltpu.CompilerParams(vmem_limit_bytes=32 << 20),
         name="solve",
-    )(slabs)
+    )(mine, theirs)
 
 
 def gathered(descriptors, positions, species, counts, w_in, b_in, w_hid, b_hid, w_out):
@@ -325,15 +332,22 @@
     ]
     slabs = pl.pallas_call(
         slab_kernel,
-        out_shape=jax.ShapeDtypeStruct((cells, ROWS, slots), jnp.float32),
+        out_shape=jax.ShapeDtypeStruct((cells // SIDES, ROWS, slots), jnp.float32),
         in_specs=[pl.BlockSpec(memory_space=pltpu.HBM)] * len(args),
         out_specs=vmem,
         scratch_shapes=landed + [pltpu.SemaphoreType.DMA((len(args),))],
         compiler_params=pltpu.CompilerParams(vmem_limit_bytes=60 << 20),
         name="slab",
     )(*args)
-    slabs = lax.all_to_all(slabs, ("cell", "sub"), 0, 0, tiled=True)
-    charges = solve_only(slabs)
+    groups = [
+        [row * columns + column for row in range(rows) for column in range(side, columns, SIDES)]
+        for side in range(SIDES)
+    ]
+    mine = lax.all_to_all(
+        slabs, ("cell", "sub"), 0, 0, tiled=True, axis_index_groups=groups
+    )
+    theirs = lax.ppermute(mine, "sub", [(column, column ^ 1) for column in range(columns)])
+    charges = solve_only(mine, theirs)
     return charges.reshape(members, 1, 1, slots)
 
 
@@ -483,7 +497,7 @@
     )
     rows, columns = mesh.shape["cell"], mesh.shape["sub"]
     return jax.shard_map(
-        gathered if sum(pair_counts(rows, columns)) <= MOST_BLOCKS else body,
+        gathered if columns % SIDES == 0 and sum(pair_counts(rows, columns)) <= MOST_BLOCKS else body,
         mesh=mesh,
         in_specs=placed,
         out_specs=P(None, ("rep", "cell"), "sub", None),

time: 26.2 us -> 25.5 us (0.973)
  blocking collectives: 16.4 us -> 14.4 us
  waiting for transfers between devices: 0 us -> 1.3 us
    all_to_all x1, blocking collectives: 16.4 us -> 14.4 us  [gathered(): lax.all_to_all(slabs, ('cell', 'sub'), 0, 0, tiled=True, axis_index_group...]
    ppermute x0 -> x1, waiting for transfers between devices: none -> 1.3 us  [gathered(): lax.ppermute(mine, 'sub', [(column, column ^ 1) for column in range(colum...]
  transfers between devices with their start and end apart: 0 -> 1, of which waited for: 0 -> 1; matrix products, arithmetic and copies ran while one was open for 0% -> 0% of each run, Pallas kernels for 0% -> 0%
where the time goes in v6:
time: 25.5 us; the launch traced here: 25.2 us
  blocking collectives  14.4 us (56%)
  Pallas kernels  8.86 us (35%)
  waiting for transfers between devices  1.3 us (5%)
  between operations  0.66 us (3%)
    all_to_all x1, blocking collectives, gathered(): lax.all_to_all(slabs, ('cell', 'sub'), 0, 0, tiled=True, axis_index_group...  14.4 us
    pallas_call x1, Pallas kernels, solve_only(): pl.pallas_call(lambda *refs: solve_kernel((rows, columns), *refs), out_sh...  6.24 us
    pallas_call x1, Pallas kernels, gathered(): pl.pallas_call(slab_kernel, out_shape=jax.ShapeDtypeStruct((cells // SIDE...  2.62 us
    ppermute x1, waiting for transfers between devices, gathered(): lax.ppermute(mine, 'sub', [(column, column ^ 1) for column in range(colum...  1.3 us
  transfers between devices with their start and end apart: 1, of which 1 were waited for; matrix products, arithmetic and copies ran while one was open for 0% of the time, Pallas kernels for 0%

profile of v6, /device:TPU:0, one launch (start us, length us, event | category | flops | bytes accessed | tf_op | source)
XLA Modules:
  0.0 25.2 jit_solution(8122156647394113256)
XLA Ops:
  0.7 2.6 %slab.1 = f32[8,24,128]{2,1,0:T(8,128)} custom-call(bf16[128,128]{1,0:T(8,128)(2,1)} %bitcast.4, f32[3,1,1,128]{3,2,1,0:T(1,128)} %refs_1_.1, s32[1,1,128]{2,1,0:T(1,128)} %refs_2_.1, s32[1,1]{1,0:T(1,128)S(6)} %copy.11.refs_3_, bf16[8,128,256]{2,1,0:T(8,128)(2,1)} %refs_4_.1, f32[8,256]{1,0:T(8,128)} %refs_5_.1, bf16[8,256,256]{2,1,0:T(8,128)(2,1)} %refs_6_.1, ...), custom_call_target="tpu_custom_call" | custom-call | tf_op jit(solution)/shard_map/slab/pallas_call | solution.py:333
  3.3 14.4 %all_to_all.5.refs_0_ = f32[8,24,128]{2,1,0:T(8,128)S(1)} all-to-all(f32[8,24,128]{2,1,0:T(8,128)} %slab.1), channel_id=1, replica_groups={{0,2,4,6,8,10,12,14},{1,3,5,7,9,11,13,15},{16,18,20,22,24,26,28,30},{17..., dimensions={0} | all-to-all | bytes 196608 | tf_op jit(solution)/shard_map/all_to_all | solution.py:346
  17.7 0.0 collective-permute-start
  17.7 1.3 %collective-permute-done.refs_1_ = f32[8,24,128]{2,1,0:T(8,128)S(1)} collective-permute-done((f32[8,24,128]{2,1,0:T(8,128)S(1)}, f32[8,24,128]{2,1,0:T(8,128)S(1)}, u32[]{:S(2)}, u32[]{:S(2)}) %collective-permute-start) | collective-permute-done | bytes 98336 | tf_op jit(solution)/shard_map/ppermute | solution.py:349
  19.0 6.2 %solve.1 = f32[8,128]{1,0:T(8,128)} custom-call(f32[8,24,128]{2,1,0:T(8,128)S(1)} %all_to_all.5.refs_0_, f32[8,24,128]{2,1,0:T(8,128)S(1)} %collective-permute-done.refs_1_), custom_call_target="tpu_custom_call" | custom-call | tf_op jit(solution)/shard_map/solve/pallas_call | solution.py:302
Async XLA Ops:
  17.7 1.3 %collective-permute-start = (f32[8,24,128]{2,1,0:T(8,128)S(1)}, f32[8,24,128]{2,1,0:T(8,128)S(1)}, u32[]{:S(2)}, u32[]{:S(2)}) collective-permute-start(f32[8,24,128]{2,1,0:T(8,128)S(1)} %all_to_all.5.refs_0_), channel_id=1, source_target_pairs={{0,1},{1,0},{2,3},{3,2},{4,5},{5,4},{6,7},{7,6},{8,9},{9,8},{10,11... | collective-permute-start | bytes 294920 | tf_op jit(solution)/shard_map/ppermute | solution.py:349

commit v7 on v6

--- a/solution.py
+++ b/solution.py
@@ -332,7 +332,7 @@
     ]
     slabs = pl.pallas_call(
         slab_kernel,
-        out_shape=jax.ShapeDtypeStruct((cells // SIDES, ROWS, slots), jnp.float32),
+        out_shape=pltpu.VMEM((cells // SIDES, ROWS, slots), jnp.float32),
         in_specs=[pl.BlockSpec(memory_space=pltpu.HBM)] * len(args),
         out_specs=vmem,
         scratch_shapes=landed + [pltpu.SemaphoreType.DMA((len(args),))],

time: 25.5 us -> 24.5 us (0.961)
  Pallas kernels: 8.86 us -> 8.22 us
    pallas_call x1, Pallas kernels: 2.62 us -> 1.98 us  [gathered(): pl.pallas_call(slab_kernel, out_shape=pltpu.VMEM((cells // SIDES, ROWS, s...]
where the time goes in v7:
time: 24.5 us; the launch traced here: 24.4 us
  blocking collectives  14.2 us (58%)
  Pallas kernels  8.22 us (34%)
  waiting for transfers between devices  1.3 us (5%)
  between operations  0.66 us (3%)
    all_to_all x1, blocking collectives, gathered(): lax.all_to_all(slabs, ('cell', 'sub'), 0, 0, tiled=True, axis_index_group...  14.2 us
    pallas_call x1, Pallas kernels, solve_only(): pl.pallas_call(lambda *refs: solve_kernel((rows, columns), *refs), out_sh...  6.24 us
    pallas_call x1, Pallas kernels, gathered(): pl.pallas_call(slab_kernel, out_shape=pltpu.VMEM((cells // SIDES, ROWS, s...  1.98 us
    ppermute x1, waiting for transfers between devices, gathered(): lax.ppermute(mine, 'sub', [(column, column ^ 1) for column in range(colum...  1.3 us
  transfers between devices with their start and end apart: 1, of which 1 were waited for; matrix products, arithmetic and copies ran while one was open for 0% of the time, Pallas kernels for 0%

profile of v7, /device:TPU:0, one launch (start us, length us, event | category | flops | bytes accessed | tf_op | source)
XLA Modules:
  0.0 24.4 jit_solution(7088130386811966431)
XLA Ops:
  0.7 2.0 %slab.1 = f32[8,24,128]{2,1,0:T(8,128)S(1)} custom-call(bf16[128,128]{1,0:T(8,128)(2,1)} %bitcast.4, f32[3,1,1,128]{3,2,1,0:T(1,128)} %refs_1_.1, s32[1,1,128]{2,1,0:T(1,128)} %refs_2_.1, s32[1,1]{1,0:T(1,128)S(6)} %copy.11.refs_3_, bf16[8,128,256]{2,1,0:T(8,128)(2,1)} %refs_4_.1, f32[8,256]{1,0:T(8,128)} %refs_5_.1, bf16[8,256,256]{2,1,0:T(8,128)(2,1)} %refs_6_.1, ...), custom_call_target="tpu_custom_call" | custom-call | tf_op jit(solution)/shard_map/slab/pallas_call | solution.py:333
  2.6 14.2 %all_to_all.5.refs_0_ = f32[8,24,128]{2,1,0:T(8,128)S(1)} all-to-all(f32[8,24,128]{2,1,0:T(8,128)S(1)} %slab.1), channel_id=1, replica_groups={{0,2,4,6,8,10,12,14},{1,3,5,7,9,11,13,15},{16,18,20,22,24,26,28,30},{17..., dimensions={0} | all-to-all | bytes 196608 | tf_op jit(solution)/shard_map/all_to_all | solution.py:346
  16.8 0.0 collective-permute-start
  16.8 1.3 %collective-permute-done.refs_1_ = f32[8,24,128]{2,1,0:T(8,128)S(1)} collective-permute-done((f32[8,24,128]{2,1,0:T(8,128)S(1)}, f32[8,24,128]{2,1,0:T(8,128)S(1)}, u32[]{:S(2)}, u32[]{:S(2)}) %collective-permute-start) | collective-permute-done | bytes 98336 | tf_op jit(solution)/shard_map/ppermute | solution.py:349
  18.1 6.2 %solve.1 = f32[8,128]{1,0:T(8,128)} custom-call(f32[8,24,128]{2,1,0:T(8,128)S(1)} %all_to_all.5.refs_0_, f32[8,24,128]{2,1,0:T(8,128)S(1)} %collective-permute-done.refs_1_), custom_call_target="tpu_custom_call" | custom-call | tf_op jit(solution)/shard_map/solve/pallas_call | solution.py:302
Async XLA Ops:
  16.8 1.3 %collective-permute-start = (f32[8,24,128]{2,1,0:T(8,128)S(1)}, f32[8,24,128]{2,1,0:T(8,128)S(1)}, u32[]{:S(2)}, u32[]{:S(2)}) collective-permute-start(f32[8,24,128]{2,1,0:T(8,128)S(1)} %all_to_all.5.refs_0_), channel_id=1, source_target_pairs={{0,1},{1,0},{2,3},{3,2},{4,5},{5,4},{6,7},{7,6},{8,9},{9,8},{10,11... | collective-permute-start | bytes 294920 | tf_op jit(solution)/shard_map/ppermute | solution.py:349

commit v8 on v7

--- a/solution.py
+++ b/solution.py
@@ -1,3 +1,5 @@
+import functools
+
 import jax
 import jax.numpy as jnp
 from jax import lax
@@ -25,7 +27,6 @@
 SQUARE, FEATURES = 24, 48
 OFFSETS = ((0, 0), (0, 1), (1, -1), (1, 0), (1, 1))
 MOST_BLOCKS = 128
-CHUNK = 128
 LAG = 12
 GROUP = 8
 SIDES = 2
@@ -161,82 +162,99 @@
     return high, (values - high.astype(jnp.float32)).astype(jnp.bfloat16)
 
 
-def solve_kernel(
-    grid, mine_ref, theirs_ref, out_ref, slab_ref, feats, near, far, vecs, sums, resid, resid_half, blocks
-):
+def grid_pairs(rows, columns):
+    pairs = []
+    for a in range(rows):
+        for da, db in OFFSETS:
+            for column in range(max(0, -db), columns - max(0, db)):
+                c = a * columns + column
+                if a + da < rows:
+                    pairs.append((c, c + da * columns + db))
+    return pairs
+
+
+def same_side(pair):
+    return pair[0] % SIDES == pair[1] % SIDES
+
+
+def views(*sides):
+    return [sides[c % len(sides)].at[c // len(sides)] for c in range(len(sides) * sides[0].shape[0])]
+
+
+def prepare(grid, source, slab, feats, near, far, vecs, sums):
     rows, columns = grid
-    cells, _, slots = slab_ref.shape
-    members = HARD
+    half, slots = columns // SIDES, slab.shape[2]
     side = lax.rem(lax.axis_index("sub"), SIDES)
-    for k in range(cells // SIDES):
-        slab_ref[SIDES * k + side] = mine_ref[k]
-        slab_ref[SIDES * k + (1 - side)] = theirs_ref[k]
+    for k in range(slab.shape[0]):
+        h = k % half
+        slab[k] = source[k + side * (half - 1 - 2 * h)]
     centres = (rows / 2, columns / 2, 0.5)
     rows_of = pair_features(
-        [slab_ref[:, PLACE + k, :] - centres[k] for k in range(3)], slab_ref[:, KIND, :]
+        [slab[:, PLACE + k, :] - centres[k] for k in range(3)], slab[:, KIND, :]
     )
     for k, row in enumerate(rows_of[0] + rows_of[1]):
         feats[:, k, :] = row
     blank = jnp.zeros((SQUARE, slots), jnp.float32)
-    for c in range(cells):
+    for c in range(slab.shape[0]):
         near[c] = feats[c, 0:FEATURES, :].T.astype(jnp.bfloat16)
         apart = jnp.concatenate([feats[c, FEATURES : FEATURES + SQUARE, :], blank], axis=0)
         spread = jnp.concatenate([blank, feats[c, FEATURES + SQUARE :, :]], axis=0)
         far[c] = jnp.concatenate([apart, spread], axis=1).astype(jnp.bfloat16)
-        high, low = halves(slab_ref[c, 0:HARD, :])
-        full = slab_ref[c, FULL : FULL + 1, :]
+        high, low = halves(slab[c, 0:HARD, :])
+        full = slab[c, FULL : FULL + 1, :]
         row = lax.broadcasted_iota(jnp.int32, (16, slots), 0)
         lines = [high.astype(jnp.float32), low.astype(jnp.float32), jnp.where(row == 0, full, 0.0)]
         lines = jnp.concatenate(lines, axis=0).astype(jnp.bfloat16)
         vecs[c] = jnp.concatenate([lines, lines], axis=1)
         sums[c] = jnp.zeros_like(sums[c])
 
-    def row_pairs(a, last):
-        pairs = []
-        for da, db in OFFSETS[:2] if last else OFFSETS:
-            for column in range(max(0, -db), columns - max(0, db)):
-                c = a * columns + column
-                place = a * (5 * columns - 3) + len(pairs)
-                pairs.append((c, c + da * columns + db, place, da == db == 0))
-        return pairs
-
-    def over_rows(handle, carry):
-        for a in range(rows):
-            carry = handle(row_pairs(a, a == rows - 1), carry)
-        return carry
-
-    def build(pairs, carry):
-        for c, d, place, own in pairs:
-            for first_row in range(0, slots, CHUNK):
-                products = times(near[c, first_row : first_row + CHUNK, :], far[d])
-                high, low = halves(pair_block(products, first_row, own))
-                blocks[place, first_row : first_row + CHUNK, :] = high
-                blocks[place, slots + first_row : slots + first_row + CHUNK, :] = low
-        return carry
-
-    def first_pass(pairs, carry):
-        terms = []
-        for c, d, place, own in pairs:
-            block = blocks[place]
-            terms.append((d, times(vecs[c], block)))
-            if not own:
-                image = times_t(vecs[d, :, 0:slots], block)
-                terms.append((c, image[:, 0:slots] + image[:, slots:]))
-        for cell, term in terms:
-            sums[cell] += term
-        return carry
-
-    every = over_rows(lambda pairs, kept: kept + pairs, [])
-    for i in range(len(every) + LAG):
-        if i >= LAG:
-            first_pass(every[i - LAG : i - LAG + 1], 0)
-        build(every[i : i + 1], 0)
+
+def build_and_apply(pairs, blocks, near, far, vecs, sums):
+    slots = near[0].shape[0]
+    lag = min(LAG, len(pairs) // 2)
+    for i in range(len(pairs) + lag):
+        if i >= lag:
+            c, d = pairs[i - lag]
+            block = blocks[i - lag]
+            image = times(vecs[c][...], block)
+            if c != d:
+                back = times_t(vecs[d][:, 0:slots], block)
+                sums[c][...] += back[:, 0:slots] + back[:, slots:]
+            sums[d][...] += image
+        if i < len(pairs):
+            c, d = pairs[i]
+            high, low = halves(pair_block(times(near[c][...], far[d][...]), 0, c == d))
+            blocks[i, 0:slots, :] = high
+            blocks[i, slots:, :] = low
+
+
+def early_kernel(grid, mine, slab, near, far, vecs, sums, blocks, feats):
+    prepare(grid, mine, slab, feats, near, far, vecs, sums)
+    pairs = [(c // SIDES, d // SIDES) for c, d in grid_pairs(*grid) if same_side((c, d)) and c % SIDES == 0]
+    build_and_apply(pairs, blocks, *(views(ref) for ref in (near, far, vecs, sums)))
+
+
+def late_kernel(
+    grid, mine_slab, mine_near, mine_far, mine_vecs, mine_sums, mine_blocks, theirs, out_ref,
+    slab, near, far, vecs, sums, sums_kept, resid, resid_half, blocks, feats
+):
+    rows, columns = grid
+    cells, members, slots = rows * columns, HARD, slab.shape[2]
+    prepare(grid, theirs, slab, feats, near, far, vecs, sums)
+    sums_kept[...] = mine_sums[...]
+    slab_of, sums_of = views(mine_slab, slab), views(sums_kept, sums)
+    every = grid_pairs(rows, columns)
+    early = [pair for pair in every if same_side(pair) and pair[0] % SIDES == 0]
+    late = [pair for pair in every if pair not in early]
+    build_and_apply(
+        late, blocks, views(mine_near, near), views(mine_far, far), views(mine_vecs, vecs), sums_of
+    )
 
     def applied(c):
-        hard = slab_ref[c, HARD:PLACE, :]
-        full = slab_ref[c, FULL : FULL + 1, :]
-        right = slab_ref[c, 0:HARD, :]
-        coupled = sums[c]
+        hard = slab_of[c][HARD:PLACE, :]
+        full = slab_of[c][FULL : FULL + 1, :]
+        right = slab_of[c][0:HARD, :]
+        coupled = sums_of[c][...]
         image_s = hard * right + full * (coupled[0:8] + coupled[8:16])
         image_u = full * (hard + coupled[16:17])
         return hard, full, right, image_s, image_u
@@ -273,14 +291,11 @@
         prod1 += jnp.concatenate([hard, hard], axis=0) * square
         total1 += left
 
-    def second_pass(pairs, carry):
-        for c, d, place, own in pairs:
-            image = times(resid_half[c], blocks[place])
-            part = (image[0:16] + image[16:32]) * resid[d]
-            carry = carry + (part if own else 2.0 * part)
-        return carry
-
-    prod1 = over_rows(second_pass, prod1)
+    for pair, block in [*zip(early, views(mine_blocks)), *zip(late, views(blocks))]:
+        c, d = pair
+        image = times(resid_half[c], block[...])
+        part = (image[0:16] + image[16:32]) * resid[d]
+        prod1 = prod1 + (part if c == d else 2.0 * part)
 
     norm1, prod1, total1 = over(norm1), over(prod1), over(total1)
     momentum = norm1 / norm0
@@ -288,36 +303,56 @@
     weight0 = alpha0 + alpha1 * momentum
     totals = weight0 * total0 + alpha1 * total1
     multiplier = totals[0:members] / totals[members:]
-    mine = lax.axis_index("cell") * columns + lax.axis_index("sub")
-    right = both(slab_ref[mine, 0:HARD, :], slab_ref[mine, FULL : FULL + 1, :])
-    answer = weight0 * right + alpha1 * resid[mine]
+    half, column = columns // SIDES, lax.axis_index("sub")
+    side, h = lax.rem(column, SIDES), lax.div(column, SIDES)
+    own = lax.axis_index("cell") * half + h + side * (half - 1 - 2 * h)
+    right = both(mine_slab[own, 0:HARD, :], mine_slab[own, FULL : FULL + 1, :])
+    answer = weight0 * right + alpha1 * resid[SIDES * own]
     out_ref[...] = answer[0:members] - multiplier * answer[members:]
 
 
 def solve_only(mine, theirs):
-    rows, columns = lax.axis_size("cell"), lax.axis_size("sub")
+    grid = rows, columns = lax.axis_size("cell"), lax.axis_size("sub")
     cells, slots = rows * columns, mine.shape[2]
+    side = cells // SIDES
+    every = grid_pairs(rows, columns)
+    early = len([pair for pair in every if same_side(pair) and pair[0] % SIDES == 0])
     vmem = pl.BlockSpec(memory_space=pltpu.VMEM)
-    blocks = sum(pair_counts(rows, columns))
+    limit = pltpu.CompilerParams(vmem_limit_bytes=32 << 20)
+    kept = [
+        pltpu.VMEM((side, ROWS, slots), jnp.float32),
+        pltpu.VMEM((side, slots, FEATURES), jnp.bfloat16),
+        pltpu.VMEM((side, FEATURES, 2 * slots), jnp.bfloat16),
+        pltpu.VMEM((side, 32, 2 * slots), jnp.bfloat16),
+        pltpu.VMEM((side, 32, slots), jnp.float32),
+    ]
+    feats = pltpu.VMEM((side, 2 * FEATURES, slots), jnp.float32)
+    begun = pl.pallas_call(
+        functools.partial(early_kernel, grid),
+        out_shape=[*kept, pltpu.VMEM((early, 2 * slots, slots), jnp.bfloat16)],
+        in_specs=[vmem],
+        out_specs=[vmem] * (len(kept) + 1),
+        scratch_shapes=[feats],
+        compiler_params=limit,
+        cost_estimate=pl.CostEstimate(flops=10**9, bytes_accessed=4 * 10**6, transcendentals=0),
+        name="early",
+    )(mine)
     return pl.pallas_call(
-        lambda *refs: solve_kernel((rows, columns), *refs),
+        functools.partial(late_kernel, grid),
         out_shape=jax.ShapeDtypeStruct((HARD, slots), jnp.float32),
-        in_specs=[vmem] * SIDES,
+        in_specs=[vmem] * (len(begun) + 1),
         out_specs=vmem,
         scratch_shapes=[
-            pltpu.VMEM((cells, ROWS, slots), jnp.float32),
-            pltpu.VMEM((cells, 2 * FEATURES, slots), jnp.float32),
-            pltpu.VMEM((cells, slots, FEATURES), jnp.bfloat16),
-            pltpu.VMEM((cells, FEATURES, 2 * slots), jnp.bfloat16),
-            pltpu.VMEM((cells, 32, 2 * slots), jnp.bfloat16),
-            pltpu.VMEM((cells, 32, slots), jnp.float32),
+            *kept,
+            pltpu.VMEM((side, 32, slots), jnp.float32),
             pltpu.VMEM((cells, 16, slots), jnp.float32),
             pltpu.VMEM((cells, 32, 2 * slots), jnp.bfloat16),
-            pltpu.VMEM((blocks, 2 * slots, slots), jnp.bfloat16),
+            pltpu.VMEM((len(every) - early, 2 * slots, slots), jnp.bfloat16),
+            feats,
         ],
-        compiler_params=pltpu.CompilerParams(vmem_limit_bytes=32 << 20),
-        name="solve",
-    )(mine, theirs)
+        compiler_params=limit,
+        name="late",
+    )(*begun, theirs)
 
 
 def gathered(descriptors, positions, species, counts, w_in, b_in, w_hid, b_hid, w_out):

time: 24.5 us -> 23.7 us (0.967)
  waiting for transfers between devices: 1.3 us -> 0.01 us
  Pallas kernels: 8.22 us -> 8.56 us
    ppermute x1, waiting for transfers between devices: 1.3 us -> 0.01 us  [gathered(): lax.ppermute(mine, 'sub', [(column, column ^ 1) for column in range(colum...]
    pallas_call x1 -> x2, Pallas kernels: 6.24 us -> 6.58 us  [the longest x1 5.11 us: solve_only(): pl.pallas_call(functools.partial(late_kernel, grid), out_shape=jax.ShapeD...]
  transfers between devices with their start and end apart: 1 -> 1, of which waited for: 1 -> 0; matrix products, arithmetic and copies ran while one was open for 0% -> 0% of each run, Pallas kernels for 0% -> 6%
where the time goes in v8:
time: 23.7 us; the launch traced here: 23.4 us
  blocking collectives  14.2 us (60%)
  Pallas kernels  8.56 us (36%)
  between operations  0.68 us (3%)
    all_to_all x1, blocking collectives, gathered(): lax.all_to_all(slabs, ('cell', 'sub'), 0, 0, tiled=True, axis_index_group...  14.2 us
    pallas_call x1, Pallas kernels, solve_only(): pl.pallas_call(functools.partial(late_kernel, grid), out_shape=jax.ShapeD...  5.11 us
    pallas_call x1, Pallas kernels, gathered(): pl.pallas_call(slab_kernel, out_shape=pltpu.VMEM((cells // SIDES, ROWS, s...  1.98 us
    pallas_call x1, Pallas kernels, solve_only(): pl.pallas_call(functools.partial(early_kernel, grid), out_shape=[*kept, p...  1.46 us
  transfers between devices with their start and end apart: 1, of which 0 were waited for; matrix products, arithmetic and copies ran while one was open for 0% of the time, Pallas kernels for 6%

profile of v8, /device:TPU:0, one launch (start us, length us, event | category | flops | bytes accessed | tf_op | source)
XLA Modules:
  0.0 23.4 jit_solution(14900269198346596910)
XLA Ops:
  0.7 2.0 %slab.1 = f32[8,24,128]{2,1,0:T(8,128)S(1)} custom-call(bf16[128,128]{1,0:T(8,128)(2,1)} %bitcast.4, f32[3,1,1,128]{3,2,1,0:T(1,128)} %refs_1_.1, s32[1,1,128]{2,1,0:T(1,128)} %refs_2_.1, s32[1,1]{1,0:T(1,128)S(6)} %copy.11.refs_3_, bf16[8,128,256]{2,1,0:T(8,128)(2,1)} %refs_4_.1, f32[8,256]{1,0:T(8,128)} %refs_5_.1, bf16[8,256,256]{2,1,0:T(8,128)(2,1)} %refs_6_.1, ...), custom_call_target="tpu_custom_call" | custom-call | tf_op jit(solution)/shard_map/slab/pallas_call | solution.py:368
  2.6 14.2 %all_to_all.5.mine = f32[8,24,128]{2,1,0:T(8,128)S(1)} all-to-all(f32[8,24,128]{2,1,0:T(8,128)S(1)} %slab.1), channel_id=1, replica_groups={{0,2,4,6,8,10,12,14},{1,3,5,7,9,11,13,15},{16,18,20,22,24,26,28,30},{17..., dimensions={0} | all-to-all | bytes 196608 | tf_op jit(solution)/shard_map/all_to_all | solution.py:381
  16.8 0.0 collective-permute-start
  16.8 1.5 %early.1 = (f32[8,24,128]{2,1,0:T(8,128)S(1)}, bf16[8,128,48]{2,1,0:T(8,128)(2,1)S(1)}, bf16[8,48,256]{2,1,0:T(8,128)(2,1)S(1)}, bf16[8,32,256]{2,1,0:T(8,128)(2...) custom-call(f32[8,24,128]{2,1,0:T(8,128)S(1)} %all_to_all.5.mine), custom_call_target="tpu_custom_call" | custom-call | flops 1000000000 | bytes 4000000 | tf_op jit(solution)/shard_map/early/pallas_call | solution.py:330
  18.3 0.0 collective-permute-done.theirs
  18.3 5.1 %late.1 = f32[8,128]{1,0:T(8,128)} custom-call(f32[8,24,128]{2,1,0:T(8,128)S(1)} %get-tuple-element.11.mine_slab, bf16[8,128,48]{2,1,0:T(8,128)(2,1)S(1)} %get-tuple-element.12.mine_near, bf16[8,48,256]{2,1,0:T(8,128)(2,1)S(1)} %get-tuple-element.13.mine_far, bf16[8,32,256]{2,1,0:T(8,128)(2,1)S(1)} %get-tuple-element.14.mine_vecs, ...), custom_call_target="tpu_custom_call" | custom-call | tf_op jit(solution)/shard_map/late/pallas_call | solution.py:340
Async XLA Ops:
  16.8 1.5 %collective-permute-start = (f32[8,24,128]{2,1,0:T(8,128)S(1)}, f32[8,24,128]{2,1,0:T(8,128)S(1)}, u32[]{:S(2)}, u32[]{:S(2)}) collective-permute-start(f32[8,24,128]{2,1,0:T(8,128)S(1)} %all_to_all.5.mine), channel_id=1, source_target_pairs={{0,1},{1,0},{2,3},{3,2},{4,5},{5,4},{6,7},{7,6},{8,9},{9,8},{10,11... | collective-permute-start | bytes 294920 | tf_op jit(solution)/shard_map/ppermute | solution.py:384

commit v9 on v8

--- a/solution.py
+++ b/solution.py
@@ -27,7 +27,9 @@
 SQUARE, FEATURES = 24, 48
 OFFSETS = ((0, 0), (0, 1), (1, -1), (1, 0), (1, 1))
 MOST_BLOCKS = 128
-LAG = 12
+LAG = 8
+AHEAD = 2
+CHUNK = 16
 GROUP = 8
 SIDES = 2
 
@@ -173,18 +175,33 @@
     return pairs
 
 
-def same_side(pair):
-    return pair[0] % SIDES == pair[1] % SIDES
-
-
-def views(*sides):
-    return [sides[c % len(sides)].at[c // len(sides)] for c in range(len(sides) * sides[0].shape[0])]
+def colour(c, columns):
+    return (c // columns + c % columns) % SIDES
+
+
+def split_pairs(rows, columns):
+    every = grid_pairs(rows, columns)
+    early = [pair for pair in every if not any(colour(c, columns) for c in pair)]
+    return early, [pair for pair in every if pair not in early]
+
+
+def items(ref):
+    return [ref.at[k] for k in range(ref.shape[0])]
+
+
+def views(columns, *sides):
+    cells = SIDES * sides[0].shape[0]
+    return [sides[colour(c, columns)].at[c // SIDES] for c in range(cells)]
+
+
+def my_side():
+    return lax.rem(lax.axis_index("cell") + lax.axis_index("sub"), SIDES)
 
 
 def prepare(grid, source, slab, feats, near, far, vecs, sums):
     rows, columns = grid
     half, slots = columns // SIDES, slab.shape[2]
-    side = lax.rem(lax.axis_index("sub"), SIDES)
+    side = my_side()
     for k in range(slab.shape[0]):
         h = k % half
         slab[k] = source[k + side * (half - 1 - 2 * h)]
@@ -209,46 +226,51 @@
         sums[c] = jnp.zeros_like(sums[c])
 
 
-def build_and_apply(pairs, blocks, near, far, vecs, sums):
+def build_and_apply(pairs, blocks, near, far, vecs, sums, products):
     slots = near[0].shape[0]
     lag = min(LAG, len(pairs) // 2)
-    for i in range(len(pairs) + lag):
-        if i >= lag:
-            c, d = pairs[i - lag]
-            block = blocks[i - lag]
+    for i in range(len(pairs) + AHEAD + lag):
+        if i < len(pairs):
+            c, d = pairs[i]
+            products[i % (AHEAD + 1)] = times(near[c][...], far[d][...])
+        k = i - AHEAD - lag
+        if k >= 0:
+            c, d = pairs[k]
+            block = blocks[k]
             image = times(vecs[c][...], block)
             if c != d:
-                back = times_t(vecs[d][:, 0:slots], block)
-                sums[c][...] += back[:, 0:slots] + back[:, slots:]
+                wide = jnp.concatenate([block[0:slots], block[slots:]], axis=1)
+                sums[c][...] += times_t(vecs[d][...], wide)
             sums[d][...] += image
-        if i < len(pairs):
-            c, d = pairs[i]
-            high, low = halves(pair_block(times(near[c][...], far[d][...]), 0, c == d))
-            blocks[i, 0:slots, :] = high
-            blocks[i, slots:, :] = low
-
-
-def early_kernel(grid, mine, slab, near, far, vecs, sums, blocks, feats):
+        k = i - AHEAD
+        if 0 <= k < len(pairs):
+            c, d = pairs[k]
+            for row in range(0, slots, CHUNK):
+                part = products[k % (AHEAD + 1), row : row + CHUNK, :]
+                high, low = halves(pair_block(part, row, c == d))
+                blocks[k, row : row + CHUNK, :] = high
+                blocks[k, slots + row : slots + row + CHUNK, :] = low
+
+
+def early_kernel(grid, mine, slab, near, far, vecs, sums, blocks, feats, products):
     prepare(grid, mine, slab, feats, near, far, vecs, sums)
-    pairs = [(c // SIDES, d // SIDES) for c, d in grid_pairs(*grid) if same_side((c, d)) and c % SIDES == 0]
-    build_and_apply(pairs, blocks, *(views(ref) for ref in (near, far, vecs, sums)))
+    pairs = [(c // SIDES, d // SIDES) for c, d in split_pairs(*grid)[0]]
+    build_and_apply(pairs, blocks, *map(items, (near, far, vecs, sums)), products)
 
 
 def late_kernel(
     grid, mine_slab, mine_near, mine_far, mine_vecs, mine_sums, mine_blocks, theirs, out_ref,
-    slab, near, far, vecs, sums, sums_kept, resid, resid_half, blocks, feats
+    slab, near, far, vecs, sums, sums_kept, resid, resid_half, blocks, feats, products
 ):
     rows, columns = grid
     cells, members, slots = rows * columns, HARD, slab.shape[2]
     prepare(grid, theirs, slab, feats, near, far, vecs, sums)
     sums_kept[...] = mine_sums[...]
-    slab_of, sums_of = views(mine_slab, slab), views(sums_kept, sums)
-    every = grid_pairs(rows, columns)
-    early = [pair for pair in every if same_side(pair) and pair[0] % SIDES == 0]
-    late = [pair for pair in every if pair not in early]
-    build_and_apply(
-        late, blocks, views(mine_near, near), views(mine_far, far), views(mine_vecs, vecs), sums_of
-    )
+    slab_of, sums_of = views(columns, mine_slab, slab), views(columns, sums_kept, sums)
+    early, late = split_pairs(rows, columns)
+    held = ((mine_near, near), (mine_far, far), (mine_vecs, vecs))
+    sides = [views(columns, *pair) for pair in held]
+    build_and_apply(late, blocks, *sides, sums_of, products)
 
     def applied(c):
         hard = slab_of[c][HARD:PLACE, :]
@@ -291,7 +313,7 @@
         prod1 += jnp.concatenate([hard, hard], axis=0) * square
         total1 += left
 
-    for pair, block in [*zip(early, views(mine_blocks)), *zip(late, views(blocks))]:
+    for pair, block in [*zip(early, items(mine_blocks)), *zip(late, items(blocks))]:
         c, d = pair
         image = times(resid_half[c], block[...])
         part = (image[0:16] + image[16:32]) * resid[d]
@@ -303,11 +325,12 @@
     weight0 = alpha0 + alpha1 * momentum
     totals = weight0 * total0 + alpha1 * total1
     multiplier = totals[0:members] / totals[members:]
-    half, column = columns // SIDES, lax.axis_index("sub")
-    side, h = lax.rem(column, SIDES), lax.div(column, SIDES)
-    own = lax.axis_index("cell") * half + h + side * (half - 1 - 2 * h)
+    half, row, side = columns // SIDES, lax.axis_index("cell"), my_side()
+    h = lax.div(lax.axis_index("sub"), SIDES)
+    h = h + side * (half - 1 - 2 * h)
+    own, cell = row * half + h, row * columns + SIDES * h + lax.rem(row, SIDES)
     right = both(mine_slab[own, 0:HARD, :], mine_slab[own, FULL : FULL + 1, :])
-    answer = weight0 * right + alpha1 * resid[SIDES * own]
+    answer = weight0 * right + alpha1 * resid[cell]
     out_ref[...] = answer[0:members] - multiplier * answer[members:]
 
 
@@ -315,8 +338,7 @@
     grid = rows, columns = lax.axis_size("cell"), lax.axis_size("sub")
     cells, slots = rows * columns, mine.shape[2]
     side = cells // SIDES
-    every = grid_pairs(rows, columns)
-    early = len([pair for pair in every if same_side(pair) and pair[0] % SIDES == 0])
+    early, late = map(len, split_pairs(rows, columns))
     vmem = pl.BlockSpec(memory_space=pltpu.VMEM)
     limit = pltpu.CompilerParams(vmem_limit_bytes=32 << 20)
     kept = [
@@ -326,13 +348,16 @@
         pltpu.VMEM((side, 32, 2 * slots), jnp.bfloat16),
         pltpu.VMEM((side, 32, slots), jnp.float32),
     ]
-    feats = pltpu.VMEM((side, 2 * FEATURES, slots), jnp.float32)
+    work = [
+        pltpu.VMEM((side, 2 * FEATURES, slots), jnp.float32),
+        pltpu.VMEM((AHEAD + 1, slots, 2 * slots), jnp.float32),
+    ]
     begun = pl.pallas_call(
         functools.partial(early_kernel, grid),
         out_shape=[*kept, pltpu.VMEM((early, 2 * slots, slots), jnp.bfloat16)],
         in_specs=[vmem],
         out_specs=[vmem] * (len(kept) + 1),
-        scratch_shapes=[feats],
+        scratch_shapes=work,
         compiler_params=limit,
         cost_estimate=pl.CostEstimate(flops=10**9, bytes_accessed=4 * 10**6, transcendentals=0),
         name="early",
@@ -347,8 +372,8 @@
             pltpu.VMEM((side, 32, slots), jnp.float32),
             pltpu.VMEM((cells, 16, slots), jnp.float32),
             pltpu.VMEM((cells, 32, 2 * slots), jnp.bfloat16),
-            pltpu.VMEM((len(every) - early, 2 * slots, slots), jnp.bfloat16),
-            feats,
+            pltpu.VMEM((late, 2 * slots, slots), jnp.bfloat16),
+            *work,
         ],
         compiler_params=limit,
         name="late",
@@ -375,8 +400,7 @@
         name="slab",
     )(*args)
     groups = [
-        [row * columns + column for row in range(rows) for column in range(side, columns, SIDES)]
-        for side in range(SIDES)
+        [c for c in range(cells) if colour(c, columns) == side] for side in range(SIDES)
     ]
     mine = lax.all_to_all(
         slabs, ("cell", "sub"), 0, 0, tiled=True, axis_index_groups=groups

time: 23.7 us -> 23 us (0.970)
  blocking collectives: 14.2 us -> 13 us
  starting transfers between devices: 0.01 us -> 0.68 us
    all_to_all x1, blocking collectives: 14.2 us -> 13 us  [gathered(): lax.all_to_all(slabs, ('cell', 'sub'), 0, 0, tiled=True, axis_index_group...]
    ppermute x1, starting transfers between devices: 0.01 us -> 0.68 us  [gathered(): lax.ppermute(mine, 'sub', [(column, column ^ 1) for column in range(colum...]
    pallas_call x1, Pallas kernels: 5.11 us -> 4.81 us  [solve_only(): pl.pallas_call(functools.partial(late_kernel, grid), out_shape=jax.ShapeD...]
  transfers between devices with their start and end apart: 1 -> 1, of which waited for: 0 -> 0; matrix products, arithmetic and copies ran while one was open for 0% -> 0% of each run, Pallas kernels for 6% -> 7%
where the time goes in v9:
time: 23 us; the launch traced here: 22.8 us
  blocking collectives  13 us (57%)
  Pallas kernels  8.44 us (37%)
  starting transfers between devices  0.68 us (3%)
  between operations  0.68 us (3%)
    all_to_all x1, blocking collectives, gathered(): lax.all_to_all(slabs, ('cell', 'sub'), 0, 0, tiled=True, axis_index_group...  13 us
    pallas_call x1, Pallas kernels, solve_only(): pl.pallas_call(functools.partial(late_kernel, grid), out_shape=jax.ShapeD...  4.81 us
    pallas_call x1, Pallas kernels, gathered(): pl.pallas_call(slab_kernel, out_shape=pltpu.VMEM((cells // SIDES, ROWS, s...  1.98 us
    pallas_call x1, Pallas kernels, solve_only(): pl.pallas_call(functools.partial(early_kernel, grid), out_shape=[*kept, p...  1.65 us
    ppermute x1, starting transfers between devices, gathered(): lax.ppermute(mine, 'sub', [(column, column ^ 1) for column in range(colum...  0.68 us
  transfers between devices with their start and end apart: 1, of which 0 were waited for; matrix products, arithmetic and copies ran while one was open for 0% of the time, Pallas kernels for 7%

profile of v9, /device:TPU:0, one launch (start us, length us, event | category | flops | bytes accessed | tf_op | source)
XLA Modules:
  0.0 22.8 jit_solution(2250144541592455703)
XLA Ops:
  0.7 2.0 %slab.1 = f32[8,24,128]{2,1,0:T(8,128)S(1)} custom-call(bf16[128,128]{1,0:T(8,128)(2,1)} %bitcast.4, f32[3,1,1,128]{3,2,1,0:T(1,128)} %refs_1_.1, s32[1,1,128]{2,1,0:T(1,128)} %refs_2_.1, s32[1,1]{1,0:T(1,128)S(6)} %copy.11.refs_3_, bf16[8,128,256]{2,1,0:T(8,128)(2,1)} %refs_4_.1, f32[8,256]{1,0:T(8,128)} %refs_5_.1, bf16[8,256,256]{2,1,0:T(8,128)(2,1)} %refs_6_.1, ...), custom_call_target="tpu_custom_call" | custom-call | tf_op jit(solution)/shard_map/slab/pallas_call | solution.py:393
  2.6 13.0 %all_to_all.5.mine = f32[8,24,128]{2,1,0:T(8,128)S(1)} all-to-all(f32[8,24,128]{2,1,0:T(8,128)S(1)} %slab.1), channel_id=1, replica_groups={{0,2,5,7,8,10,13,15},{1,3,4,6,9,11,12,14},{16,18,21,23,24,26,29,31},{17..., dimensions={0} | all-to-all | bytes 196608 | tf_op jit(solution)/shard_map/all_to_all | solution.py:405
  15.7 0.7 %collective-permute-start = (f32[8,24,128]{2,1,0:T(8,128)S(1)}, f32[8,24,128]{2,1,0:T(8,128)S(1)}, u32[]{:S(2)}, u32[]{:S(2)}) collective-permute-start(f32[8,24,128]{2,1,0:T(8,128)S(1)} %all_to_all.5.mine), channel_id=1, source_target_pairs={{0,1},{1,0},{2,3},{3,2},{4,5},{5,4},{6,7},{7,6},{8,9},{9,8},{10,11... | collective-permute-start | bytes 294920 | tf_op jit(solution)/shard_map/ppermute | solution.py:408
  16.4 1.7 %early.1 = (f32[8,24,128]{2,1,0:T(8,128)S(1)}, bf16[8,128,48]{2,1,0:T(8,128)(2,1)S(1)}, bf16[8,48,256]{2,1,0:T(8,128)(2,1)S(1)}, bf16[8,32,256]{2,1,0:T(8,128)(2...) custom-call(f32[8,24,128]{2,1,0:T(8,128)S(1)} %all_to_all.5.mine), custom_call_target="tpu_custom_call" | custom-call | flops 1000000000 | bytes 4000000 | tf_op jit(solution)/shard_map/early/pallas_call | solution.py:355
  18.0 0.0 collective-permute-done.theirs
  18.0 4.8 %late.1 = f32[8,128]{1,0:T(8,128)} custom-call(f32[8,24,128]{2,1,0:T(8,128)S(1)} %get-tuple-element.11.mine_slab, bf16[8,128,48]{2,1,0:T(8,128)(2,1)S(1)} %get-tuple-element.12.mine_near, bf16[8,48,256]{2,1,0:T(8,128)(2,1)S(1)} %get-tuple-element.13.mine_far, bf16[8,32,256]{2,1,0:T(8,128)(2,1)S(1)} %get-tuple-element.14.mine_vecs, ...), custom_call_target="tpu_custom_call" | custom-call | tf_op jit(solution)/shard_map/late/pallas_call | solution.py:365
Async XLA Ops:
  15.7 2.3 %collective-permute-start = (f32[8,24,128]{2,1,0:T(8,128)S(1)}, f32[8,24,128]{2,1,0:T(8,128)S(1)}, u32[]{:S(2)}, u32[]{:S(2)}) collective-permute-start(f32[8,24,128]{2,1,0:T(8,128)S(1)} %all_to_all.5.mine), channel_id=1, source_target_pairs={{0,1},{1,0},{2,3},{3,2},{4,5},{5,4},{6,7},{7,6},{8,9},{9,8},{10,11... | collective-permute-start | bytes 294920 | tf_op jit(solution)/shard_map/ppermute | solution.py:408

commit v10 on v9

--- a/solution.py
+++ b/solution.py
@@ -286,6 +286,7 @@
     norm_u = jnp.zeros((1, slots), jnp.float32)
     for c in range(cells):
         hard, full, right, image_s, image_u = applied(c)
+        resid[c] = jnp.concatenate([image_s, image_u], axis=0)
         norm_s += right * right
         norm_u += full * full
         prod_s += right * image_s
@@ -302,8 +303,9 @@
 
     norm1, prod1, total1 = (jnp.zeros((2 * members, slots), jnp.float32) for _ in range(3))
     for c in range(cells):
-        hard, full, right, image_s, image_u = applied(c)
-        left = both(right, full) - alpha0 * jnp.concatenate([image_s, image_u], axis=0)
+        hard = slab_of[c][HARD:PLACE, :]
+        right, full = slab_of[c][0:HARD, :], slab_of[c][FULL : FULL + 1, :]
+        left = both(right, full) - alpha0 * resid[c]
         resid[c] = left
         high, low = halves(left)
         lines = jnp.concatenate([high, low], axis=0)
@@ -313,11 +315,16 @@
         prod1 += jnp.concatenate([hard, hard], axis=0) * square
         total1 += left
 
-    for pair, block in [*zip(early, items(mine_blocks)), *zip(late, items(blocks))]:
-        c, d = pair
-        image = times(resid_half[c], block[...])
-        part = (image[0:16] + image[16:32]) * resid[d]
-        prod1 = prod1 + (part if c == d else 2.0 * part)
+    stored = dict(zip(early + late, items(mine_blocks) + items(blocks)))
+    for c in range(cells):
+        others = [d for b, d in stored if b == c]
+        for first in range(0, len(others), 2):
+            some = others[first : first + 2]
+            image = times(resid_half[c], jnp.concatenate([stored[c, d][...] for d in some], axis=1))
+            for k, d in enumerate(some):
+                part = image[:, k * slots : (k + 1) * slots]
+                part = (part[0:16] + part[16:32]) * resid[d]
+                prod1 = prod1 + (part if c == d else 2.0 * part)
 
     norm1, prod1, total1 = over(norm1), over(prod1), over(total1)
     momentum = norm1 / norm0

time: 23 us -> 23 us (level)
  no operation moved by 1% of the time
where the time goes in v10:
time: 23 us; the launch traced here: 22.8 us
  blocking collectives  13 us (57%)
  Pallas kernels  8.44 us (37%)
  starting transfers between devices  0.68 us (3%)
  between operations  0.68 us (3%)
    all_to_all x1, blocking collectives, gathered(): lax.all_to_all(slabs, ('cell', 'sub'), 0, 0, tiled=True, axis_index_group...  13 us
    pallas_call x1, Pallas kernels, solve_only(): pl.pallas_call(functools.partial(late_kernel, grid), out_shape=jax.ShapeD...  4.8 us
    pallas_call x1, Pallas kernels, gathered(): pl.pallas_call(slab_kernel, out_shape=pltpu.VMEM((cells // SIDES, ROWS, s...  1.98 us
    pallas_call x1, Pallas kernels, solve_only(): pl.pallas_call(functools.partial(early_kernel, grid), out_shape=[*kept, p...  1.65 us
    ppermute x1, starting transfers between devices, gathered(): lax.ppermute(mine, 'sub', [(column, column ^ 1) for column in range(colum...  0.68 us
  transfers between devices with their start and end apart: 1, of which 0 were waited for; matrix products, arithmetic and copies ran while one was open for 0% of the time, Pallas kernels for 7%

profile of v10, /device:TPU:0, one launch (start us, length us, event | category | flops | bytes accessed | tf_op | source)
XLA Modules:
  0.0 22.8 jit_solution(1456405760693240907)
XLA Ops:
  0.7 2.0 %slab.1 = f32[8,24,128]{2,1,0:T(8,128)S(1)} custom-call(bf16[128,128]{1,0:T(8,128)(2,1)} %bitcast.4, f32[3,1,1,128]{3,2,1,0:T(1,128)} %refs_1_.1, s32[1,1,128]{2,1,0:T(1,128)} %refs_2_.1, s32[1,1]{1,0:T(1,128)S(6)} %copy.11.refs_3_, bf16[8,128,256]{2,1,0:T(8,128)(2,1)} %refs_4_.1, f32[8,256]{1,0:T(8,128)} %refs_5_.1, bf16[8,256,256]{2,1,0:T(8,128)(2,1)} %refs_6_.1, ...), custom_call_target="tpu_custom_call" | custom-call | tf_op jit(solution)/shard_map/slab/pallas_call | solution.py:400
  2.6 13.0 %all_to_all.5.mine = f32[8,24,128]{2,1,0:T(8,128)S(1)} all-to-all(f32[8,24,128]{2,1,0:T(8,128)S(1)} %slab.1), channel_id=1, replica_groups={{0,2,5,7,8,10,13,15},{1,3,4,6,9,11,12,14},{16,18,21,23,24,26,29,31},{17..., dimensions={0} | all-to-all | bytes 196608 | tf_op jit(solution)/shard_map/all_to_all | solution.py:412
  15.7 0.7 %collective-permute-start = (f32[8,24,128]{2,1,0:T(8,128)S(1)}, f32[8,24,128]{2,1,0:T(8,128)S(1)}, u32[]{:S(2)}, u32[]{:S(2)}) collective-permute-start(f32[8,24,128]{2,1,0:T(8,128)S(1)} %all_to_all.5.mine), channel_id=1, source_target_pairs={{0,1},{1,0},{2,3},{3,2},{4,5},{5,4},{6,7},{7,6},{8,9},{9,8},{10,11... | collective-permute-start | bytes 294920 | tf_op jit(solution)/shard_map/ppermute | solution.py:415
  16.4 1.7 %early.1 = (f32[8,24,128]{2,1,0:T(8,128)S(1)}, bf16[8,128,48]{2,1,0:T(8,128)(2,1)S(1)}, bf16[8,48,256]{2,1,0:T(8,128)(2,1)S(1)}, bf16[8,32,256]{2,1,0:T(8,128)(2...) custom-call(f32[8,24,128]{2,1,0:T(8,128)S(1)} %all_to_all.5.mine), custom_call_target="tpu_custom_call" | custom-call | flops 1000000000 | bytes 4000000 | tf_op jit(solution)/shard_map/early/pallas_call | solution.py:362
  18.0 0.0 collective-permute-done.theirs
  18.0 4.8 %late.1 = f32[8,128]{1,0:T(8,128)} custom-call(f32[8,24,128]{2,1,0:T(8,128)S(1)} %get-tuple-element.11.mine_slab, bf16[8,128,48]{2,1,0:T(8,128)(2,1)S(1)} %get-tuple-element.12.mine_near, bf16[8,48,256]{2,1,0:T(8,128)(2,1)S(1)} %get-tuple-element.13.mine_far, bf16[8,32,256]{2,1,0:T(8,128)(2,1)S(1)} %get-tuple-element.14.mine_vecs, ...), custom_call_target="tpu_custom_call" | custom-call | tf_op jit(solution)/shard_map/late/pallas_call | solution.py:372
Async XLA Ops:
  15.7 2.3 %collective-permute-start = (f32[8,24,128]{2,1,0:T(8,128)S(1)}, f32[8,24,128]{2,1,0:T(8,128)S(1)}, u32[]{:S(2)}, u32[]{:S(2)}) collective-permute-start(f32[8,24,128]{2,1,0:T(8,128)S(1)} %all_to_all.5.mine), channel_id=1, source_target_pairs={{0,1},{1,0},{2,3},{3,2},{4,5},{5,4},{6,7},{7,6},{8,9},{9,8},{10,11... | collective-permute-start | bytes 294920 | tf_op jit(solution)/shard_map/ppermute | solution.py:415

commit v11 on v10

--- a/solution.py
+++ b/solution.py
@@ -32,6 +32,7 @@
 CHUNK = 16
 GROUP = 8
 SIDES = 2
+HELD = 24
 
 
 def pair_counts(rows, cols):
@@ -143,9 +144,9 @@
         value = value * y + 0.005 * term
     value = value * ((left * inv) * (left * left))
     if own:
-        i = lax.broadcasted_iota(jnp.int32, value.shape, 0) + first_row
+        i = lax.broadcasted_iota(jnp.int32, value.shape, 0)
         j = lax.broadcasted_iota(jnp.int32, value.shape, 1)
-        value = jnp.where(i == j, 0.0, value)
+        value = jnp.where(j - i == first_row, 0.0, value)
     return value
 
 
@@ -240,8 +241,8 @@
             image = times(vecs[c][...], block)
             if c != d:
                 wide = jnp.concatenate([block[0:slots], block[slots:]], axis=1)
-                sums[c][...] += times_t(vecs[d][...], wide)
-            sums[d][...] += image
+                sums[c][...] += times_t(vecs[d][...], wide)[0:HELD]
+            sums[d][...] += image[0:HELD]
         k = i - AHEAD
         if 0 <= k < len(pairs):
             c, d = pairs[k]
@@ -353,7 +354,7 @@
         pltpu.VMEM((side, slots, FEATURES), jnp.bfloat16),
         pltpu.VMEM((side, FEATURES, 2 * slots), jnp.bfloat16),
         pltpu.VMEM((side, 32, 2 * slots), jnp.bfloat16),
-        pltpu.VMEM((side, 32, slots), jnp.float32),
+        pltpu.VMEM((side, HELD, slots), jnp.float32),
     ]
     work = [
         pltpu.VMEM((side, 2 * FEATURES, slots), jnp.float32),
@@ -376,7 +377,7 @@
         out_specs=vmem,
         scratch_shapes=[
             *kept,
-            pltpu.VMEM((side, 32, slots), jnp.float32),
+            pltpu.VMEM((side, HELD, slots), jnp.float32),
             pltpu.VMEM((cells, 16, slots), jnp.float32),
             pltpu.VMEM((cells, 32, 2 * slots), jnp.bfloat16),
             pltpu.VMEM((late, 2 * slots, slots), jnp.bfloat16),

time: 23 us -> 23 us (level)
  no operation moved by 1% of the time
where the time goes in v11:
time: 23 us; the launch traced here: 22.8 us
  blocking collectives  13 us (57%)
  Pallas kernels  8.42 us (37%)
  starting transfers between devices  0.68 us (3%)
  between operations  0.68 us (3%)
    all_to_all x1, blocking collectives, gathered(): lax.all_to_all(slabs, ('cell', 'sub'), 0, 0, tiled=True, axis_index_group...  13 us
    pallas_call x1, Pallas kernels, solve_only(): pl.pallas_call(functools.partial(late_kernel, grid), out_shape=jax.ShapeD...  4.79 us
    pallas_call x1, Pallas kernels, gathered(): pl.pallas_call(slab_kernel, out_shape=pltpu.VMEM((cells // SIDES, ROWS, s...  1.98 us
    pallas_call x1, Pallas kernels, solve_only(): pl.pallas_call(functools.partial(early_kernel, grid), out_shape=[*kept, p...  1.64 us
    ppermute x1, starting transfers between devices, gathered(): lax.ppermute(mine, 'sub', [(column, column ^ 1) for column in range(colum...  0.68 us
  transfers between devices with their start and end apart: 1, of which 0 were waited for; matrix products, arithmetic and copies ran while one was open for 0% of the time, Pallas kernels for 7%

profile of v11, /device:TPU:0, one launch (start us, length us, event | category | flops | bytes accessed | tf_op | source)
XLA Modules:
  0.0 22.8 jit_solution(9458874076087647363)
XLA Ops:
  0.7 2.0 %slab.1 = f32[8,24,128]{2,1,0:T(8,128)S(1)} custom-call(bf16[128,128]{1,0:T(8,128)(2,1)} %bitcast.4, f32[3,1,1,128]{3,2,1,0:T(1,128)} %refs_1_.1, s32[1,1,128]{2,1,0:T(1,128)} %refs_2_.1, s32[1,1]{1,0:T(1,128)S(6)} %copy.11.refs_3_, bf16[8,128,256]{2,1,0:T(8,128)(2,1)} %refs_4_.1, f32[8,256]{1,0:T(8,128)} %refs_5_.1, bf16[8,256,256]{2,1,0:T(8,128)(2,1)} %refs_6_.1, ...), custom_call_target="tpu_custom_call" | custom-call | tf_op jit(solution)/shard_map/slab/pallas_call | solution.py:401
  2.6 13.0 %all_to_all.5.mine = f32[8,24,128]{2,1,0:T(8,128)S(1)} all-to-all(f32[8,24,128]{2,1,0:T(8,128)S(1)} %slab.1), channel_id=1, replica_groups={{0,2,5,7,8,10,13,15},{1,3,4,6,9,11,12,14},{16,18,21,23,24,26,29,31},{17..., dimensions={0} | all-to-all | bytes 196608 | tf_op jit(solution)/shard_map/all_to_all | solution.py:413
  15.7 0.7 %collective-permute-start = (f32[8,24,128]{2,1,0:T(8,128)S(1)}, f32[8,24,128]{2,1,0:T(8,128)S(1)}, u32[]{:S(2)}, u32[]{:S(2)}) collective-permute-start(f32[8,24,128]{2,1,0:T(8,128)S(1)} %all_to_all.5.mine), channel_id=1, source_target_pairs={{0,1},{1,0},{2,3},{3,2},{4,5},{5,4},{6,7},{7,6},{8,9},{9,8},{10,11... | collective-permute-start | bytes 294920 | tf_op jit(solution)/shard_map/ppermute | solution.py:416
  16.4 1.6 %early.1 = (f32[8,24,128]{2,1,0:T(8,128)S(1)}, bf16[8,128,48]{2,1,0:T(8,128)(2,1)S(1)}, bf16[8,48,256]{2,1,0:T(8,128)(2,1)S(1)}, bf16[8,32,256]{2,1,0:T(8,128)(2...) custom-call(f32[8,24,128]{2,1,0:T(8,128)S(1)} %all_to_all.5.mine), custom_call_target="tpu_custom_call" | custom-call | flops 1000000000 | bytes 4000000 | tf_op jit(solution)/shard_map/early/pallas_call | solution.py:363
  18.0 0.0 collective-permute-done.theirs
  18.0 4.8 %late.1 = f32[8,128]{1,0:T(8,128)} custom-call(f32[8,24,128]{2,1,0:T(8,128)S(1)} %get-tuple-element.11.mine_slab, bf16[8,128,48]{2,1,0:T(8,128)(2,1)S(1)} %get-tuple-element.12.mine_near, bf16[8,48,256]{2,1,0:T(8,128)(2,1)S(1)} %get-tuple-element.13.mine_far, bf16[8,32,256]{2,1,0:T(8,128)(2,1)S(1)} %get-tuple-element.14.mine_vecs, ...), custom_call_target="tpu_custom_call" | custom-call | tf_op jit(solution)/shard_map/late/pallas_call | solution.py:373
Async XLA Ops:
  15.7 2.3 %collective-permute-start = (f32[8,24,128]{2,1,0:T(8,128)S(1)}, f32[8,24,128]{2,1,0:T(8,128)S(1)}, u32[]{:S(2)}, u32[]{:S(2)}) collective-permute-start(f32[8,24,128]{2,1,0:T(8,128)S(1)} %all_to_all.5.mine), channel_id=1, source_target_pairs={{0,1},{1,0},{2,3},{3,2},{4,5},{5,4},{6,7},{7,6},{8,9},{9,8},{10,11... | collective-permute-start | bytes 294920 | tf_op jit(solution)/shard_map/ppermute | solution.py:416
